TPU v7x, 128 devices: a whole 4x4x4 slice. The times are simulated.
128 devices in a mesh: gx: 4 (over y), gy: 4 (over x_lo, core), gz: 8 (over z, x_hi).
Axes of the slice: x: 4 (x_hi: 2, x_lo: 2; x = x_hi * 2 + x_lo), y: 4, z: 4, core: 2. Of those that a mesh axis runs over, the one named last changes fastest.
Arguments:
- forcing: float32 [128, 128, 1024], P('gx', 'gy', 'gz'), may hold values from -6 to 6
- kappa_base: float32 [128, 128, 1024], P('gx', 'gy', 'gz'), may hold values from 0.5 to 2
- labels: int32 [128, 128, 1024], P('gx', 'gy', 'gz'), may hold values from 0 to 3
- contrast: float32 [4], replicated, may hold values from 1 to 100
- channel_weight: float32 [4], replicated, may hold values from 0.25 to 2
- coarse_coef: float32 [4, 4, 8, 64, 8], P('gx', 'gy', 'gz'), may hold values from -6 to 6
- source_link: int32 [4, 4, 8, 40, 4], P('gx', 'gy', 'gz'), may hold values from 0 to 63, as said below
- offsets: int32 [4, 4, 8, 40, 3], P('gx', 'gy', 'gz'), may hold values from 0 to 120, as said below
- live_pieces: int32 [4, 4, 8], P('gx', 'gy', 'gz'), may hold values from 5 to 40, as said below
- resident_bases: float32 [4, 4, 8, 40, 8, 4096], P('gx', 'gy', 'gz'), may hold values from -5 to 5
Outputs:
- update: float32 [128, 128, 1024], P('gx', 'gy', 'gz')
- new_basis: float32 [4, 4, 8, 40, 2, 4096], P('gx', 'gy', 'gz')
Inputs may be any that keep to these rules, and one draw needn't show every extreme that they name: `source_link`: each of the three brick offsets of a slot, minus one, leads to a brick inside the mesh; a coefficient slot may be named by several pieces. `offsets`: every piece lies inside its brick's padded frame of (40) x (40) x (136) cells. `live_pieces`: some brick has all 40 slots live in every draw.
All inputs are finite; a program needn't handle non-finite values.
Results may differ from a plain program's by a relative error of at most 0.0003.
Values sent between devices are 32-bit elements; how exact they have to be, the bound alone decides.
A program may use at most 128 MiB of HBM per device.

v0:
```python
import jax
import jax.numpy as jnp
from jax import lax
from jax.sharding import PartitionSpec as P

BX = 32
BY = 32
BZ = 128
MARGIN = 4
PIECE = 16
NB = 8
NP = 40
ND = 64
SWEEPS = 20
BLOCK = 8


damping = 2.0 / 3.0


def extended(array, sides, width):
    for axis, dim in sides:
        count, length = (lax.axis_size(axis), array.shape[dim])
        up = [(i, (i + 1) % count) for i in range(count - 1)]
        down = [(j, i) for i, j in up]
        last = lax.slice_in_dim(array, length - width, length, axis=dim)
        leading = lax.slice_in_dim(array, 0, width, axis=dim)
        before = lax.ppermute(last, axis, up)
        after = lax.ppermute(leading, axis, down)
        array = jnp.concatenate([before, array, after], axis=dim)
    return array


def lookup(labels, values):
    accumulated = jnp.zeros(labels.shape, values.dtype)
    for channel in range(values.shape[0]):
        accumulated = accumulated + jnp.where(labels == channel, values[channel], 0.0)
    return accumulated


def neighbour(array, axis_number, offset_step):
    selection = [slice(1, -1), slice(1, -1), slice(1, -1)]
    extent = array.shape[axis_number]
    selection[axis_number] = slice(1 + offset_step, extent - 1 + offset_step)
    return array[tuple(selection)]


def apply_operator(values, conductivity, inside):
    centre = values[1:-1, 1:-1, 1:-1]
    centre_kappa = conductivity[1:-1, 1:-1, 1:-1]
    accumulated = jnp.zeros_like(centre)
    for axis_number in range(3):
        for offset_step in (-1, 1):
            beside_values = neighbour(values, axis_number, offset_step)
            beside_kappa = neighbour(conductivity, axis_number, offset_step)
            beside_inside = neighbour(inside, axis_number, offset_step)
            face_value = jnp.where(
                beside_inside > 0, 0.5 * (centre_kappa + beside_kappa), centre_kappa
            )
            accumulated = accumulated + face_value * (centre - beside_values)
    return accumulated


def shift_flat(values, stride, upward):
    filler = jnp.zeros(values.shape[:-1] + (stride,), values.dtype)
    if upward:
        return jnp.concatenate([values[..., stride:], filler], -1)
    return jnp.concatenate([filler, values[..., :-stride]], -1)


def local_solve(sources, conductivity, inside):
    flat_index = jnp.arange(PIECE**3)
    couplings = []
    diagonal = jnp.zeros_like(conductivity)
    for stride in (PIECE * PIECE, PIECE, 1):
        grid_position = flat_index // stride % PIECE
        for upward, allowed in ((True, grid_position < PIECE - 1), (False, grid_position > 0)):
            beside_kappa = shift_flat(conductivity, stride, upward)
            beside_inside = shift_flat(inside, stride, upward) * allowed.astype(inside.dtype)
            face_value = jnp.where(
                beside_inside > 0, 0.5 * (conductivity + beside_kappa), conductivity
            )
            diagonal = diagonal + face_value
            couplings.append((stride, upward, jnp.where(beside_inside > 0, face_value, 0.0)))
    divisor = jnp.where(inside > 0, diagonal, 1.0)

    def sweep(sweep_index, solution):
        gathered_terms = jnp.zeros_like(solution)
        for stride, upward, coupling in couplings:
            gathered_terms = gathered_terms + coupling[:, None, :] * shift_flat(
                solution, stride, upward
            )
        update_term = sources - (diagonal[:, None, :] * solution - gathered_terms)
        return solution + damping * inside[:, None, :] * update_term / divisor[:, None, :]

    return lax.fori_loop(0, SWEEPS, sweep, jnp.zeros_like(sources))


def tent_weights():
    flat_index = jnp.arange(PIECE**3)
    product = jnp.ones((PIECE**3,), jnp.float32)
    for stride in (PIECE * PIECE, PIECE, 1):
        grid_position = (flat_index // stride % PIECE).astype(jnp.float32)
        product = (
            product
            * (grid_position + 0.5)
            * (PIECE - grid_position - 0.5)
            * (4.0 / (PIECE * PIECE))
        )
    return product


def axis_mask(position, extent, depth, whole_extent):
    cells = position * extent - depth + jnp.arange(extent + 2 * depth)
    return ((cells >= 0) & (cells < whole_extent)).astype(jnp.float32)


def domain_mask(depth):
    along_x = axis_mask(lax.axis_index("gx"), BX, depth, BX * lax.axis_size("gx"))
    along_y = axis_mask(lax.axis_index("gy"), BY, depth, BY * lax.axis_size("gy"))
    along_z = axis_mask(lax.axis_index("gz"), BZ, depth, BZ * lax.axis_size("gz"))
    return along_x[:, None, None] * along_y[None, :, None] * along_z[None, None, :]


def fold_margins(field_with_halo):
    halo_width = MARGIN
    holder_array = jnp.concatenate([field_with_halo[:halo_width], field_with_halo[-halo_width:]], 0)
    widened_region = extended(holder_array, (("gx", 0),), halo_width)
    inner_region = field_with_halo[halo_width:-halo_width]
    inner_region = (
        inner_region.at[:halo_width]
        .add(widened_region[:halo_width])
        .at[-halo_width:]
        .add(widened_region[-halo_width:])
    )
    holder_array = jnp.concatenate([inner_region[:, :halo_width], inner_region[:, -halo_width:]], 1)
    widened_region = extended(holder_array, (("gy", 1),), halo_width)
    central_part = inner_region[:, halo_width:-halo_width]
    central_part = (
        central_part.at[:, :halo_width]
        .add(widened_region[:, :halo_width])
        .at[:, -halo_width:]
        .add(widened_region[:, -halo_width:])
    )
    holder_array = jnp.concatenate(
        [central_part[:, :, :halo_width], central_part[:, :, -halo_width:]], 2
    )
    widened_region = extended(holder_array, (("gz", 2),), halo_width)
    inner = central_part[:, :, halo_width:-halo_width]
    inner = (
        inner.at[:, :, :halo_width]
        .add(widened_region[:, :, :halo_width])
        .at[:, :, -halo_width:]
        .add(widened_region[:, :, -halo_width:])
    )
    return inner


def corner_cell(corner_block, member):
    return (corner_block[member, 0], corner_block[member, 1], corner_block[member, 2])


def local(
    forcing,
    kappa_base,
    labels,
    contrast,
    channel_weight,
    coarse_coef,
    source_link,
    offsets,
    live_pieces,
    resident_bases,
):
    piece_cells = PIECE**3
    cube_shape = (PIECE, PIECE, PIECE)
    padded_shape = (BX + 2 * MARGIN, BY + 2 * MARGIN, BZ + 2 * MARGIN)
    kappa = kappa_base * lookup(labels, contrast)
    weight = lookup(labels, channel_weight)
    link_table = source_link[0, 0, 0]
    everything = lax.all_gather(
        coarse_coef.reshape(1, ND, NB), ("gx", "gy", "gz"), axis=0, tiled=True
    )
    source_number = (
        (
            (lax.axis_index("gx") + link_table[:, 0] - 1) * lax.axis_size("gy")
            + lax.axis_index("gy")
            + link_table[:, 1]
            - 1
        )
        * lax.axis_size("gz")
        + lax.axis_index("gz")
        + link_table[:, 2]
        - 1
    )
    coef_rows = everything[source_number, link_table[:, 3]]
    live_count = live_pieces[0, 0, 0]
    count_of_blocks = (live_count + BLOCK - 1) // BLOCK
    corner_table = offsets[0, 0, 0]
    basis_table = resident_bases[0, 0, 0]

    def prolong(block_index, field_with_halo):
        first_slot = block_index * BLOCK
        coef_block = lax.dynamic_slice_in_dim(coef_rows, first_slot, BLOCK, 0)
        basis_block = lax.dynamic_slice_in_dim(basis_table, first_slot, BLOCK, 0)
        corner_block = lax.dynamic_slice_in_dim(corner_table, first_slot, BLOCK, 0)
        active = (first_slot + jnp.arange(BLOCK) < live_count).astype(jnp.float32)
        values = (
            jnp.einsum("pk,pkc->pc", coef_block, basis_block, precision=lax.Precision.HIGHEST)
            * active[:, None]
        )
        for member in range(BLOCK):
            start_cell = corner_cell(corner_block, member)
            existing = lax.dynamic_slice(field_with_halo, start_cell, cube_shape)
            field_with_halo = lax.dynamic_update_slice(
                field_with_halo, existing + values[member].reshape(cube_shape), start_cell
            )
        return field_with_halo

    partial_field = lax.fori_loop(0, count_of_blocks, prolong, jnp.zeros(padded_shape, jnp.float32))
    coarse_field = fold_margins(partial_field)
    field_ext, kappa_ext = (
        extended(coarse_field, (("gx", 0), ("gy", 1), ("gz", 2)), 1),
        extended(kappa, (("gx", 0), ("gy", 1), ("gz", 2)), 1),
    )
    residual = forcing - apply_operator(field_ext, kappa_ext, domain_mask(1))
    residual_pad, kappa_pad, weight_pad = (
        extended(residual, (("gx", 0), ("gy", 1), ("gz", 2)), MARGIN),
        extended(kappa, (("gx", 0), ("gy", 1), ("gz", 2)), MARGIN),
        extended(weight, (("gx", 0), ("gy", 1), ("gz", 2)), MARGIN),
    )
    inside_pad = domain_mask(MARGIN)
    tent = tent_weights()

    def enrich(block_index, carried):
        correction, basis_out = carried
        first_slot = block_index * BLOCK
        corner_block = lax.dynamic_slice_in_dim(corner_table, first_slot, BLOCK, 0)
        active = (first_slot + jnp.arange(BLOCK) < live_count).astype(jnp.float32)
        collected = ([], [], [], [])
        for member in range(BLOCK):
            start_cell = corner_cell(corner_block, member)
            for target, source_field in zip(
                collected, (residual_pad, kappa_pad, weight_pad, inside_pad)
            ):
                target.append(
                    lax.dynamic_slice(source_field, start_cell, cube_shape).reshape(piece_cells)
                )
        residual_block, kappa_block, weight_block, inside_block = [
            jnp.stack(column) for column in collected
        ]
        sources = jnp.stack([residual_block, residual_block * weight_block], 1)
        solved = local_solve(sources, kappa_block, inside_block) * active[:, None, None]
        basis_out = lax.dynamic_update_slice_in_dim(basis_out, solved, first_slot, 0)
        spread = tent[None, :] * (solved[:, 0] + solved[:, 1])
        for member in range(BLOCK):
            start_cell = corner_cell(corner_block, member)
            existing = lax.dynamic_slice(correction, start_cell, cube_shape)
            correction = lax.dynamic_update_slice(
                correction, existing + spread[member].reshape(cube_shape), start_cell
            )
        return (correction, basis_out)

    initial = (jnp.zeros(padded_shape, jnp.float32), jnp.zeros((NP, 2, piece_cells), jnp.float32))
    correction, basis_out = lax.fori_loop(0, count_of_blocks, enrich, initial)
    update = coarse_field + fold_margins(correction)
    return (update, basis_out.reshape(1, 1, 1, NP, 2, piece_cells))


def solution(mesh):
    return jax.shard_map(
        local,
        mesh=mesh,
        in_specs=(
            P("gx", "gy", "gz"),
            P("gx", "gy", "gz"),
            P("gx", "gy", "gz"),
            P(),
            P(),
            P("gx", "gy", "gz", None, None),
            P("gx", "gy", "gz", None, None),
            P("gx", "gy", "gz", None, None),
            P("gx", "gy", "gz"),
            P("gx", "gy", "gz", None, None, None),
        ),
        out_specs=(P("gx", "gy", "gz"), P("gx", "gy", "gz", None, None, None)),
        check_vma=False,
    )
```

profile of v0, /device:TPU:69, one launch (start us, length us, event | category | flops | bytes accessed | tf_op | source)
XLA Modules:
  0.0 1903.2 jit_solution(330750338290088289)
XLA Ops:
  2.1 4.0 select_add_fusion
  15.5 4.0 collective-permute-start.12
  21.5 295.8 %all-gather = f32[128,1,1,64,8]{3,4,2,1,0:T(8,128)S(1)} all-gather(f32[1,1,1,64,8]{3,4,2,1,0:T(8,128)S(1)} %copy-done.30), channel_id=2, replica_groups=mesh['gx'=4,'gy'=4,'gz'=8] {'gx','gy','gz'}, dimensions={0}, use_global_device_ids=true | all-gather | bytes 264192 | tf_op jit(solution)/shard_map/all_gather | solution.py:181
  322.4 185.6 %while.60 = (s32[]{:T(128)}, f32[40,40,136]{2,1,0:T(8,128)S(1)}, s32[]{:T(128)}, s32[40,3]{0,1:T(4,128)S(1)}, f32[40,8]{1,0:T(8,128)S(1)}, /*index=5*/f32[40,8,4...) while((s32[]{:T(128)}, f32[40,40,136]{2,1,0:T(8,128)S(1)}, ...), condition=%wide.region_1.2_spmd, body=%wide.region_0.1_spmd.sunk | while | flops 3211366 | bytes 2624807 | solution.py:220
  332.7 5.3 dynamic_update_slice.114
  344.7 5.4 dynamic_update_slice.115
  356.3 5.4 dynamic_update_slice.116
  367.4 5.3 dynamic_update_slice.117
  378.4 5.4 dynamic_update_slice.118
  389.7 5.4 dynamic_update_slice.119
  400.6 5.4 dynamic_update_slice.120
  412.1 5.4 dynamic_update_slice.121
  427.8 5.4 dynamic_update_slice.114
  439.9 5.3 dynamic_update_slice.115
  451.4 5.2 dynamic_update_slice.116
  462.4 5.4 dynamic_update_slice.117
  473.4 5.4 dynamic_update_slice.118
  484.7 5.3 dynamic_update_slice.119
  502.6 5.4 dynamic_update_slice.121
  512.4 89.9 %collective-permute-start.16 = (f32[34,1,128]{2,0,1:T(8,128)S(1)}, f32[34,1,128]{2,0,1:T(8,128)S(1)}, u32[]{:S(2)}, u32[]{:S(2)}) collective-permute-start(f32[34,1,128]{2,0,1:T(8,128)S(1)} %copy.147), channel_id=1, source_target_pairs={{0,8},{8,16},{16,24},{1,9},{9,17},{17,25},{2,10},{10,18},{18,26},{... | collective-permute-start | bytes 52232 | tf_op jit(solution)/shard_map/ppermute | solution.py:28
  609.5 4.8 collective-permute-start.20
  614.6 189.4 %collective-permute-start.22 = (f32[34,34,1]{1,0,2:T(8,128)S(1)}, f32[34,34,1]{1,0,2:T(8,128)S(1)}, u32[]{:S(2)}, u32[]{:S(2)}) collective-permute-start(f32[34,34,1]{1,0,2:T(8,128)S(1)} %copy.119), channel_id=1, source_target_pairs={{1,0},{2,1},{3,2},{4,3},{5,4},{6,5},{7,6},{9,8},{10,9},{11,10},{12... | collective-permute-start | bytes 13880 | tf_op jit(solution)/shard_map/ppermute | solution.py:29
  807.4 4.6 collective-permute-start.6
  823.7 4.2 collective-permute-done.3
  836.2 7.6 collective-permute-done.4
  843.8 6.0 collective-permute-start.5
  851.4 9.0 collective-permute-done.5
  861.7 5.9 scatter-add.49
  867.6 4.3 collective-permute-start.13
  906.9 5.2 collective-permute-start.23
  916.4 5.2 collective-permute-start.35
  930.4 9.2 fusion.29
  946.2 5.4 collective-permute-start.11
  952.4 5.9 collective-permute-start.26
  976.8 5.4 collective-permute-start.29
  982.3 3.9 pad_maximum_fusion.1
  986.3 4.1 copy.135
  990.3 4.2 copy.133
  994.5 5.5 pad_maximum_fusion.2
  1000.0 4.0 copy.134
  1005.8 337.4 %while.62 = (s32[]{:T(128)}, f32[40,40,136]{2,1,0:T(8,128)S(1)}, f32[40,2,4096]{2,1,0:T(2,128)}, s32[]{:T(128)}, s32[40,3]{0,1:T(4,128)S(1)}, /*index=5*/f32[40,...) while((s32[]{:T(128)}, f32[40,40,136]{2,1,0:T(8,128)S(1)}, ...), condition=%wide.region_5.6_spmd.clone, body=%wide.region_2.5_spmd.clone.sunk | while | flops 4001897 | bytes 24314324 | solution.py:265
  1082.8 47.2 %while.63 = (s32[]{:T(128)}, f32[8,2,4096]{2,1,0:T(2,128)S(1)}, f32[8,4096]{1,0:T(8,128)S(1)}, f32[8,4096]{1,0:T(8,128)S(1)}, f32[8,4096]{1,0:T(8,128)S(1)}, /*i...) while((s32[]{:T(128)}, f32[8,2,4096]{2,1,0:T(2,128)S(1)}, ...), condition=%wide.region_4.4_spmd.clone, body=%wide.region_3.3_spmd.clone.sunk | while | flops 1277955 | bytes 7366416 | solution.py:96
  1132.5 5.3 dynamic_update_slice.123
  1138.1 5.4 dynamic_update_slice.124
  1143.7 5.4 dynamic_update_slice.125
  1149.3 5.3 dynamic_update_slice.126
  1154.8 5.4 dynamic_update_slice.127
  1160.4 5.4 dynamic_update_slice.128
  1166.0 5.4 dynamic_update_slice.129
  1171.6 5.4 dynamic_update_slice.130
  1253.5 47.2 %while.63 = (s32[]{:T(128)}, f32[8,2,4096]{2,1,0:T(2,128)S(1)}, f32[8,4096]{1,0:T(8,128)S(1)}, f32[8,4096]{1,0:T(8,128)S(1)}, f32[8,4096]{1,0:T(8,128)S(1)}, /*i...) while((s32[]{:T(128)}, f32[8,2,4096]{2,1,0:T(2,128)S(1)}, ...), condition=%wide.region_4.4_spmd.clone, body=%wide.region_3.3_spmd.clone.sunk | while | flops 1277955 | bytes 7366416 | solution.py:96
  1303.1 5.4 dynamic_update_slice.123
  1308.7 5.3 dynamic_update_slice.124
  1314.3 5.2 dynamic_update_slice.125
  1319.7 5.4 dynamic_update_slice.126
  1325.3 5.4 dynamic_update_slice.127
  1330.9 5.3 dynamic_update_slice.128
  1337.6 5.4 dynamic_update_slice.130
  1346.8 182.3 %collective-permute-done.37 = f32[4,40,136]{2,1,0:T(8,128)S(1)} collective-permute-done((f32[4,40,136]{2,1,0:T(8,128)S(1)}, f32[4,40,136]{2,1,0:T(8,128)S(1)}, u32[]{:S(2)}, u32[]{:S(2)}) %collective-permute-start.37) | collective-permute-done | bytes 87072 | tf_op jit(solution)/shard_map/ppermute | solution.py:29
  1529.3 6.2 collective-permute-start.38
  1537.8 4.3 collective-permute-done.39
  1544.5 339.8 %collective-permute-start.41 = (f32[32,32,4]{2,1,0:T(8,128)S(1)}, f32[32,32,4]{2,1,0:T(8,128)S(1)}, u32[]{:S(2)}, u32[]{:S(2)}) collective-permute-start(f32[32,32,4]{2,1,0:T(8,128)S(1)} %get-tuple-element.808), channel_id=1, source_target_pairs={{1,0},{2,1},{3,2},{4,3},{5,4},{6,5},{7,6},{9,8},{10,9},{11,10},{12... | collective-permute-start | bytes 49160 | tf_op jit(solution)/shard_map/ppermute | solution.py:29
  1884.3 10.0 collective-permute-done.40
  1896.2 5.9 scatter-add.59
  (743 shorter events, 317.9 us)
Async XLA Ops:
  0.6 11.3 copy-start.29
  0.6 12.0 copy-start.18
  2.1 19.4 %copy-start.30 = (f32[1,1,1,64,8]{3,4,2,1,0:T(8,128)S(1)}, f32[1,1,1,64,8]{3,4,2,1,0:T(8,128)}, u32[]{:S(2)}) copy-start(f32[1,1,1,64,8]{3,4,2,1,0:T(8,128)} %param.45) | copy-start | bytes 6148
  6.8 813.7 %collective-permute-start.30 = (f32[4,32,128]{2,1,0:T(8,128)}, f32[4,32,128]{2,1,0:T(8,128)}, u32[]{:S(2)}, u32[]{:S(2)}) collective-permute-start(f32[4,32,128]{2,1,0:T(8,128)} %get-tuple-element.826), channel_id=1, source_target_pairs={{0,32},{32,64},{64,96},{1,33},{33,65},{65,97},{2,34},{34,66},{66,9... | collective-permute-start | bytes 196616 | tf_op jit(solution)/shard_map/ppermute | solution.py:28
  10.6 809.9 %collective-permute-start.31 = (f32[4,32,128]{2,1,0:T(8,128)}, f32[4,32,128]{2,1,0:T(8,128)}, u32[]{:S(2)}, u32[]{:S(2)}) collective-permute-start(f32[4,32,128]{2,1,0:T(8,128)} %get-tuple-element.827), channel_id=1, source_target_pairs={{32,0},{64,32},{96,64},{33,1},{65,33},{97,65},{34,2},{66,34},{98,6... | collective-permute-start | bytes 196616 | tf_op jit(solution)/shard_map/ppermute | solution.py:29
  15.5 857.7 %copy-start.14 = (f32[32,32,128]{2,1,0:T(8,128)}, f32[32,32,128]{2,1,0:T(8,128)S(1)}, u32[]{:S(2)}) copy-start(f32[32,32,128]{2,1,0:T(8,128)S(1)} %add_multiply_fusion) | copy-start | bytes 1572868
  15.5 496.9 %collective-permute-start.12 = (f32[1,32,128]{2,1,0:T(8,128)S(1)}, f32[1,32,128]{2,1,0:T(8,128)S(1)}, u32[]{:S(2)}, u32[]{:S(2)}) collective-permute-start(f32[1,32,128]{2,1,0:T(8,128)S(1)} %get-tuple-element.830), channel_id=1, source_target_pairs={{0,32},{32,64},{64,96},{1,33},{33,65},{65,97},{2,34},{34,66},{66,9... | collective-permute-start | bytes 49160 | tf_op jit(solution)/shard_map/ppermute | solution.py:28
  19.5 492.9 %collective-permute-start.14 = (f32[1,32,128]{2,1,0:T(8,128)S(1)}, f32[1,32,128]{2,1,0:T(8,128)S(1)}, u32[]{:S(2)}, u32[]{:S(2)}) collective-permute-start(f32[1,32,128]{2,1,0:T(8,128)S(1)} %get-tuple-element.831), channel_id=1, source_target_pairs={{32,0},{64,32},{96,64},{33,1},{65,33},{97,65},{34,2},{66,34},{98,6... | collective-permute-start | bytes 49160 | tf_op jit(solution)/shard_map/ppermute | solution.py:29
  508.0 97.7 %copy-start.19 = (s32[40,3]{0,1:T(4,128)}, s32[40,3]{0,1:T(4,128)S(1)}, u32[]{:S(2)}) copy-start(s32[40,3]{0,1:T(4,128)S(1)} %get-tuple-element.1461) | copy-start | bytes 1444
  508.8 304.5 %collective-permute-start = (f32[4,40,136]{2,1,0:T(8,128)}, f32[4,40,136]{2,1,0:T(8,128)}, u32[]{:S(2)}, u32[]{:S(2)}) collective-permute-start(f32[4,40,136]{2,1,0:T(8,128)} %get-tuple-element.803), channel_id=1, source_target_pairs={{0,32},{32,64},{64,96},{1,33},{33,65},{65,97},{2,34},{34,66},{66,9... | collective-permute-start | bytes 261128 | tf_op jit(solution)/shard_map/ppermute | solution.py:28
  512.4 95.2 %copy-start.25 = (f32[1,32,128]{2,1,0:T(8,128)}, f32[1,32,128]{2,1,0:T(8,128)S(1)}, u32[]{:S(2)}) copy-start(f32[1,32,128]{2,1,0:T(8,128)S(1)} %collective-permute-done.12) | copy-start | bytes 49156
  512.4 95.2 %copy-start.27 = (f32[1,32,128]{2,1,0:T(8,128)}, f32[1,32,128]{2,1,0:T(8,128)S(1)}, u32[]{:S(2)}) copy-start(f32[1,32,128]{2,1,0:T(8,128)S(1)} %collective-permute-done.14) | copy-start | bytes 49156
  512.4 93.2 %collective-permute-start.16 = (f32[34,1,128]{2,0,1:T(8,128)S(1)}, f32[34,1,128]{2,0,1:T(8,128)S(1)}, u32[]{:S(2)}, u32[]{:S(2)}) collective-permute-start(f32[34,1,128]{2,0,1:T(8,128)S(1)} %copy.147), channel_id=1, source_target_pairs={{0,8},{8,16},{16,24},{1,9},{9,17},{17,25},{2,10},{10,18},{18,26},{... | collective-permute-start | bytes 52232 | tf_op jit(solution)/shard_map/ppermute | solution.py:28
  602.4 5.1 collective-permute-start.18
  609.5 195.3 %collective-permute-start.20 = (f32[34,34,1]{1,0,2:T(8,128)}, f32[34,34,1]{1,0,2:T(8,128)S(1)}, u32[]{:S(2)}, u32[]{:S(2)}) collective-permute-start(f32[34,34,1]{1,0,2:T(8,128)} %copy.113), channel_id=1, source_target_pairs={{0,1},{1,2},{2,3},{3,4},{4,5},{5,6},{6,7},{8,9},{9,10},{10,11},{11... | collective-permute-start | bytes 13880 | tf_op jit(solution)/shard_map/ppermute | solution.py:28
  614.6 192.8 %collective-permute-start.22 = (f32[34,34,1]{1,0,2:T(8,128)S(1)}, f32[34,34,1]{1,0,2:T(8,128)S(1)}, u32[]{:S(2)}, u32[]{:S(2)}) collective-permute-start(f32[34,34,1]{1,0,2:T(8,128)S(1)} %copy.119), channel_id=1, source_target_pairs={{1,0},{2,1},{3,2},{4,3},{5,4},{6,5},{7,6},{9,8},{10,9},{11,10},{12... | collective-permute-start | bytes 13880 | tf_op jit(solution)/shard_map/ppermute | solution.py:29
  804.8 10.8 collective-permute-start.1
  807.4 64.5 %collective-permute-start.6 = (f32[4,32,128]{2,1,0:T(8,128)}, f32[4,32,128]{2,1,0:T(8,128)}, u32[]{:S(2)}, u32[]{:S(2)}) collective-permute-start(f32[4,32,128]{2,1,0:T(8,128)} %get-tuple-element.834), channel_id=1, source_target_pairs={{0,32},{32,64},{64,96},{1,33},{33,65},{65,97},{2,34},{34,66},{66,9... | collective-permute-start | bytes 196616 | tf_op jit(solution)/shard_map/ppermute | solution.py:28
  813.2 7.3 copy-start.17
  813.2 60.0 %collective-permute-start.7 = (f32[4,32,128]{2,1,0:T(8,128)}, f32[4,32,128]{2,1,0:T(8,128)}, u32[]{:S(2)}, u32[]{:S(2)}) collective-permute-start(f32[4,32,128]{2,1,0:T(8,128)} %get-tuple-element.835), channel_id=1, source_target_pairs={{32,0},{64,32},{96,64},{33,1},{65,33},{97,65},{34,2},{66,34},{98,6... | collective-permute-start | bytes 196616 | tf_op jit(solution)/shard_map/ppermute | solution.py:29
  816.7 6.9 collective-permute-start.2
  821.7 6.3 collective-permute-start.3
  829.0 14.8 collective-permute-start.4
  831.0 59.9 %collective-permute-start.32 = (f32[40,4,128]{2,0,1:T(8,128)S(1)}, f32[40,4,128]{2,0,1:T(8,128)}, u32[]{:S(2)}, u32[]{:S(2)}) collective-permute-start(f32[40,4,128]{2,0,1:T(8,128)S(1)} %copy.153), channel_id=1, source_target_pairs={{0,8},{8,16},{16,24},{1,9},{9,17},{17,25},{2,10},{10,18},{18,26},{... | collective-permute-start | bytes 245768 | tf_op jit(solution)/shard_map/ppermute | solution.py:28
  832.9 63.0 %collective-permute-start.33 = (f32[40,4,128]{2,0,1:T(8,128)S(1)}, f32[40,4,128]{2,0,1:T(8,128)}, u32[]{:S(2)}, u32[]{:S(2)}) collective-permute-start(f32[40,4,128]{2,0,1:T(8,128)S(1)} %copy.154), channel_id=1, source_target_pairs={{8,0},{16,8},{24,16},{9,1},{17,9},{25,17},{10,2},{18,10},{26,18},{... | collective-permute-start | bytes 245768 | tf_op jit(solution)/shard_map/ppermute | solution.py:29
  843.8 16.7 collective-permute-start.5
  867.6 62.7 %copy-start.12 = (f32[32,32,128]{2,1,0:T(8,128)}, f32[32,32,128]{2,1,0:T(8,128)S(1)}, u32[]{:S(2)}) copy-start(f32[32,32,128]{2,1,0:T(8,128)S(1)} %scatter-add.49) | copy-start | bytes 1572868
  867.6 6.5 collective-permute-start.13
  871.9 4.5 collective-permute-start.15
  874.1 7.4 copy-start.15
  876.4 22.8 %collective-permute-start.17 = (f32[34,1,128]{2,0,1:T(8,128)S(1)}, f32[34,1,128]{2,0,1:T(8,128)S(1)}, u32[]{:S(2)}, u32[]{:S(2)}) collective-permute-start(f32[34,1,128]{2,0,1:T(8,128)S(1)} %copy.148), channel_id=1, source_target_pairs={{0,8},{8,16},{16,24},{1,9},{9,17},{17,25},{2,10},{10,18},{18,26},{... | collective-permute-start | bytes 52232 | tf_op jit(solution)/shard_map/ppermute | solution.py:28
  879.6 19.7 %collective-permute-start.19 = (f32[34,1,128]{2,0,1:T(8,128)}, f32[34,1,128]{2,0,1:T(8,128)}, u32[]{:S(2)}, u32[]{:S(2)}) collective-permute-start(f32[34,1,128]{2,0,1:T(8,128)} %copy.150), channel_id=1, source_target_pairs={{8,0},{16,8},{24,16},{9,1},{17,9},{25,17},{10,2},{18,10},{26,18},{... | collective-permute-start | bytes 52232 | tf_op jit(solution)/shard_map/ppermute | solution.py:29
  886.6 29.8 %collective-permute-start.8 = (f32[40,4,128]{2,0,1:T(8,128)}, f32[40,4,128]{2,0,1:T(8,128)S(1)}, u32[]{:S(2)}, u32[]{:S(2)}) collective-permute-start(f32[40,4,128]{2,0,1:T(8,128)} %copy.145), channel_id=1, source_target_pairs={{0,8},{8,16},{16,24},{1,9},{9,17},{17,25},{2,10},{10,18},{18,26},{... | collective-permute-start | bytes 245768 | tf_op jit(solution)/shard_map/ppermute | solution.py:28
  890.9 33.1 %collective-permute-start.9 = (f32[40,4,128]{2,0,1:T(8,128)}, f32[40,4,128]{2,0,1:T(8,128)}, u32[]{:S(2)}, u32[]{:S(2)}) collective-permute-start(f32[40,4,128]{2,0,1:T(8,128)} %copy.146), channel_id=1, source_target_pairs={{8,0},{16,8},{24,16},{9,1},{17,9},{25,17},{10,2},{18,10},{26,18},{... | collective-permute-start | bytes 245768 | tf_op jit(solution)/shard_map/ppermute | solution.py:29
  902.9 24.3 %collective-permute-start.21 = (f32[34,34,1]{1,0,2:T(8,128)S(1)}, f32[34,34,1]{1,0,2:T(8,128)S(1)}, u32[]{:S(2)}, u32[]{:S(2)}) collective-permute-start(f32[34,34,1]{1,0,2:T(8,128)S(1)} %copy.117), channel_id=1, source_target_pairs={{0,1},{1,2},{2,3},{3,4},{4,5},{5,6},{6,7},{8,9},{9,10},{10,11},{11... | collective-permute-start | bytes 13880 | tf_op jit(solution)/shard_map/ppermute | solution.py:28
  906.9 21.5 %collective-permute-start.23 = (f32[34,34,1]{1,0,2:T(8,128)}, f32[34,34,1]{1,0,2:T(8,128)}, u32[]{:S(2)}, u32[]{:S(2)}) collective-permute-start(f32[34,34,1]{1,0,2:T(8,128)} %copy.121), channel_id=1, source_target_pairs={{1,0},{2,1},{3,2},{4,3},{5,4},{6,5},{7,6},{9,8},{10,9},{11,10},{12... | collective-permute-start | bytes 13880 | tf_op jit(solution)/shard_map/ppermute | solution.py:29
  913.9 45.1 %collective-permute-start.34 = (f32[40,40,4]{1,0,2:T(8,128)}, f32[40,40,4]{1,0,2:T(8,128)S(1)}, u32[]{:S(2)}, u32[]{:S(2)}) collective-permute-start(f32[40,40,4]{1,0,2:T(8,128)} %get-tuple-element.794), channel_id=1, source_target_pairs={{0,1},{1,2},{2,3},{3,4},{4,5},{5,6},{6,7},{8,9},{9,10},{10,11},{11... | collective-permute-start | bytes 76808 | tf_op jit(solution)/shard_map/ppermute | solution.py:28
  916.4 44.5 %collective-permute-start.35 = (f32[40,40,4]{1,0,2:T(8,128)S(1)}, f32[40,40,4]{1,0,2:T(8,128)}, u32[]{:S(2)}, u32[]{:S(2)}) collective-permute-start(f32[40,40,4]{1,0,2:T(8,128)S(1)} %get-tuple-element.795), channel_id=1, source_target_pairs={{1,0},{2,1},{3,2},{4,3},{5,4},{6,5},{7,6},{9,8},{10,9},{11,10},{12... | collective-permute-start | bytes 76808 | tf_op jit(solution)/shard_map/ppermute | solution.py:29
  930.4 12.1 copy-start.7
  930.4 12.1 copy-start.9
  939.6 6.6 collective-permute-start.24
  941.1 10.5 collective-permute-start.25
  942.4 18.5 copy-start.4
  942.5 18.5 copy-start.5
  942.5 18.5 copy-start.6
  943.3 39.0 %collective-permute-start.10 = (f32[40,40,4]{1,0,2:T(8,128)}, f32[40,40,4]{1,0,2:T(8,128)}, u32[]{:S(2)}, u32[]{:S(2)}) collective-permute-start(f32[40,40,4]{1,0,2:T(8,128)} %get-tuple-element.798), channel_id=1, source_target_pairs={{0,1},{1,2},{2,3},{3,4},{4,5},{5,6},{6,7},{8,9},{9,10},{10,11},{11... | collective-permute-start | bytes 76808 | tf_op jit(solution)/shard_map/ppermute | solution.py:28
  946.2 36.1 %collective-permute-start.11 = (f32[40,40,4]{1,0,2:T(8,128)}, f32[40,40,4]{1,0,2:T(8,128)}, u32[]{:S(2)}, u32[]{:S(2)}) collective-permute-start(f32[40,40,4]{1,0,2:T(8,128)} %get-tuple-element.799), channel_id=1, source_target_pairs={{1,0},{2,1},{3,2},{4,3},{5,4},{6,5},{7,6},{9,8},{10,9},{11,10},{12... | collective-permute-start | bytes 76808 | tf_op jit(solution)/shard_map/ppermute | solution.py:29
  952.4 14.6 collective-permute-start.26
  959.0 11.2 collective-permute-start.27
  973.4 8.9 copy-start.8
  973.4 8.9 copy-start.10
  974.8 19.8 %collective-permute-start.28 = (f32[40,40,4]{1,0,2:T(8,128)S(1)}, f32[40,40,4]{1,0,2:T(8,128)S(1)}, u32[]{:S(2)}, u32[]{:S(2)}) collective-permute-start(f32[40,40,4]{1,0,2:T(8,128)S(1)} %get-tuple-element.796), channel_id=1, source_target_pairs={{0,1},{1,2},{2,3},{3,4},{4,5},{5,6},{6,7},{8,9},{9,10},{10,11},{11... | collective-permute-start | bytes 76808 | tf_op jit(solution)/shard_map/ppermute | solution.py:28
  976.8 17.7 collective-permute-start.29
  1074.2 7.1 copy-start
  1074.2 7.1 copy-start.1
  1074.2 7.0 copy-start.2
  1074.2 7.0 copy-start.3
  1343.3 3.5 collective-permute-start.36
  1344.7 184.5 %collective-permute-start.37 = (f32[4,40,136]{2,1,0:T(8,128)S(1)}, f32[4,40,136]{2,1,0:T(8,128)S(1)}, u32[]{:S(2)}, u32[]{:S(2)}) collective-permute-start(f32[4,40,136]{2,1,0:T(8,128)S(1)} %get-tuple-element.800), channel_id=1, source_target_pairs={{32,0},{64,32},{96,64},{33,1},{65,33},{97,65},{34,2},{66,34},{98,6... | collective-permute-start | bytes 261128 | tf_op jit(solution)/shard_map/ppermute | solution.py:29
  1529.3 8.3 collective-permute-start.38
  1535.7 6.4 collective-permute-start.39
  1542.4 352.0 %collective-permute-start.40 = (f32[32,32,4]{2,1,0:T(8,128)S(1)}, f32[32,32,4]{2,1,0:T(8,128)S(1)}, u32[]{:S(2)}, u32[]{:S(2)}) collective-permute-start(f32[32,32,4]{2,1,0:T(8,128)S(1)} %get-tuple-element.809), channel_id=1, source_target_pairs={{0,1},{1,2},{2,3},{3,4},{4,5},{5,6},{6,7},{8,9},{9,10},{10,11},{11... | collective-permute-start | bytes 49160 | tf_op jit(solution)/shard_map/ppermute | solution.py:28
  1544.5 351.5 %collective-permute-start.41 = (f32[32,32,4]{2,1,0:T(8,128)S(1)}, f32[32,32,4]{2,1,0:T(8,128)S(1)}, u32[]{:S(2)}, u32[]{:S(2)}) collective-permute-start(f32[32,32,4]{2,1,0:T(8,128)S(1)} %get-tuple-element.808), channel_id=1, source_target_pairs={{1,0},{2,1},{3,2},{4,3},{5,4},{6,5},{7,6},{9,8},{10,9},{11,10},{12... | collective-permute-start | bytes 49160 | tf_op jit(solution)/shard_map/ppermute | solution.py:29
  1894.6 7.5 copy-start.13
  (15 other events, 73.4 us)
where the time goes:
time: 1940 us; the launch traced here: 1900 us
  starting transfers between devices  734 us (38%)
  local copies, waits for them, and re-layouts  340 us (18%)
  blocking collectives  296 us (15%)
  waiting for transfers between devices  222 us (11%)
  loops' own time  186 us (10%)
  other arithmetic  118 us (6%)
    ppermute x21, starting transfers between devices, extended(): after = lax.ppermute(leading, axis, down)  580 us
    all_gather x1, blocking collectives, local(): lax.all_gather(coarse_coef.reshape(1, ND, NB), ('gx', 'gy', 'gz'), axis=0...  296 us
    ppermute x21, waiting for transfers between devices, extended(): after = lax.ppermute(leading, axis, down)  204 us
    ppermute x21, starting transfers between devices, extended(): before = lax.ppermute(last, axis, up)  153 us
    another operation x1, loops' own time, local(): correction, basis_out = lax.fori_loop(0, count_of_blocks, enrich, initial)  92.5 us
    another operation x1, loops' own time, local(): lax.fori_loop(0, count_of_blocks, prolong, jnp.zeros(padded_shape, jnp.fl...  91.5 us
    dynamic_update_slice x16, local copies, waits for them, and re-layouts, prolong(): lax.dynamic_update_slice(field_with_halo, existing + values[member].resha...  81.1 us
    dynamic_update_slice x16, local copies, waits for them, and re-layouts, enrich(): lax.dynamic_update_slice(correction, existing + spread[member].reshape(cu...  81.1 us
  transfers between devices with their start and end apart: 42, of which 9 were waited for; matrix products, arithmetic and copies ran while one was open for 10% of the time, Pallas kernels for 0%

commit v1 on v0

v1 whole, which is shorter than its diff:
```python
import jax
import jax.numpy as jnp
from jax import lax
from jax.experimental import pallas as pl
from jax.experimental.pallas import tpu as pltpu
from jax.sharding import PartitionSpec as P

BX = 32
BY = 32
BZ = 128
MARGIN = 4
ND = 64
PIECE=16; NB=8; NP=40; SWEEPS=20
OMEGA = 2.0/3.0
PAIR = 2
VM = pl.BlockSpec(memory_space=pltpu.VMEM)
SM = pl.BlockSpec(memory_space=pltpu.SMEM)
ANY = pl.BlockSpec(memory_space=pl.ANY)

def corner(off, p):
    ox = jnp.clip(off[p, 0], 0, 24)
    oy = jnp.clip(off[p, 1], 0, 24)
    oz = jnp.clip(off[p, 2], 0, 120)
    tile = (oz > 112).astype(jnp.int32)
    return ox, oy, tile, oz - 8 * tile

def rot(v, shift, axis=1):
    return pltpu.roll(v, shift, axis)

def lanes_sub():
    return lax.broadcasted_iota(jnp.int32, (8, 128), 1), lax.broadcasted_iota(jnp.int32, (8, 128), 0)

def prolong_kernel(live_ref, off, coef, basis, acc, buf, sems):
    live = jnp.minimum(live_ref[0], NP)
    def start(p, c):
        pltpu.make_async_copy(basis.at[pl.ds(p*256,256)], buf.at[pl.ds(p*256,256)], sems.at[p]).start()
        return c
    lax.fori_loop(0, live, start, 0)
    acc[...] = jnp.zeros_like(acc)
    lane, sub = lanes_sub()
    def body(p, c):
        ox, oy, tile, lo = corner(off, p)
        pltpu.make_async_copy(basis.at[pl.ds(p*256,256)], buf.at[pl.ds(p*256,256)], sems.at[p]).wait()
        inwin = (lane >= lo) & (lane < lo + 16)
        for yh in range(2):
            for xo in range(2):
                v = None
                for k in range(NB):
                    t = coef[p, k] * buf[pl.ds(p*256 + 128*xo + 8*yh + k, 8, stride=16), :]
                    v = t if v is None else v + t
                for yl in range(8):
                    r = rot(v, lax.rem(lo - 16*yl + 128, 128))
                    acc[tile, oy + 8*yh + yl, pl.ds(ox + 8*xo, 8), :] += jnp.where(inwin, r, 0.0)
        return c
    lax.fori_loop(0, live, body, 0)

def enrich_kernel(live_ref, off, R, K, W, out, corr, cbuf, vbuf, sbuf):
    live = jnp.minimum(live_ref[0], NP)
    corr[...] = jnp.zeros_like(corr)
    lane, sub = lanes_sub()
    group = lane // 16
    zpos = lane % 16
    zw = zpos < 15
    zg = zpos > 0
    yup = lane < 112
    ydn = lane >= 16
    xup = sub < 7
    xdn = sub > 0
    fz = zpos.astype(jnp.float32)
    def tentf(t):
        return (t + 0.5) * (PIECE - t - 0.5) * (4.0 / (PIECE * PIECE))
    tents = {}
    for xp in range(2):
        for yp in range(2):
            tents[xp, yp] = tentf((2*sub + xp).astype(jnp.float32)) * tentf((2*group + yp).astype(jnp.float32)) * tentf(fz)
    par = [(0,0),(0,1),(1,0),(1,1)]

    def prep(p, slot):
        ox, oy, tile, lo = corner(off, p)
        active = jnp.where(p < live, 1.0, 0.0)
        got = []
        for F in (R, K, W):
            d = {}
            for xp, yp in par:
                a = None
                for yh in range(8):
                    row = F[tile, oy + 2*yh + yp, pl.ds(ox + xp, 8, stride=2), :]
                    r = rot(row, lax.rem(16*yh - lo + 128, 128))
                    a = r if a is None else jnp.where(group == yh, r, a)
                d[xp, yp] = a
            got.append(d)
        r, k, w = got
        for i, (xp, yp) in enumerate(par):
            kc = k[xp, yp]
            nbs = [
                (rot(kc, 127), zw), (rot(kc, 1), zg),
                (k[xp, 1-yp], None),
                (rot(k[xp, 1-yp], 16 if yp == 0 else 112), ydn if yp == 0 else yup),
                (k[1-xp, yp], None),
                (rot(k[1-xp, yp], 1 if xp == 0 else 7, 0), xdn if xp == 0 else xup),
            ]
            diag = None
            cs = []
            inside = kc > 0.0
            for nb, m in nbs:
                ok = nb > 0.0
                if m is not None:
                    ok = ok & m
                face = jnp.where(ok, 0.5 * (kc + nb), kc)
                cs.append(jnp.where(ok & inside, face, 0.0))
                diag = face if diag is None else diag + face
            inv = jnp.where(inside, OMEGA / jnp.where(inside, diag, 1.0), 0.0)
            for j, cj in enumerate(cs):
                cbuf[slot, pl.ds((i*6 + j)*8, 8), :] = cj * inv
            b1 = r[xp, yp] * inv * active
            vbuf[slot, pl.ds(i*8, 8), :] = b1
            vbuf[slot, pl.ds((4+i)*8, 8), :] = b1 * w[xp, yp]

    def sweep_piece(vs, slot):
        res = []
        for s in range(2):
            v = {par[i]: vs[s*4+i] for i in range(4)}
            for i, (xp, yp) in enumerate(par):
                c = [cbuf[slot, pl.ds((i*6 + j)*8, 8), :] for j in range(6)]
                vc = v[xp, yp]
                t0 = vbuf[slot, pl.ds((4*s+i)*8, 8), :] + (1.0 - OMEGA) * vc
                t1 = c[0] * rot(vc, 127) + c[1] * rot(vc, 1)
                t2 = c[2] * v[xp, 1-yp] + c[3] * rot(v[xp, 1-yp], 16 if yp == 0 else 112)
                t3 = c[4] * v[1-xp, yp] + c[5] * rot(v[1-xp, yp], 1 if xp == 0 else 7, 0)
                res.append((t0 + t1) + (t2 + t3))
        return res

    idxs = [16*(4*yh2 + group//2) + zpos for yh2 in range(2)]
    gpar = (group % 2) == 0

    def body(g, c):
        for slot in range(PAIR):
            prep(g*PAIR + slot, slot)
        init = tuple(vbuf[slot, pl.ds(n*8, 8), :] for slot in range(PAIR) for n in range(8))
        def sweep(_, vs):
            o = []
            for slot in range(PAIR):
                o += sweep_piece(vs[slot*8:slot*8+8], slot)
            return tuple(o)
        vs = lax.fori_loop(0, SWEEPS - 1, sweep, init)
        for slot in range(PAIR):
            p = g*PAIR + slot
            ox, oy, tile, lo = corner(off, p)
            inwin = (lane >= lo) & (lane < lo + 16)
            v = vs[slot*8:slot*8+8]
            for s in range(2):
                for xp in range(2):
                    for yh2 in range(2):
                        e = jnp.take_along_axis(v[s*4 + 2*xp], idxs[yh2], axis=1)
                        o = jnp.take_along_axis(v[s*4 + 2*xp + 1], idxs[yh2], axis=1)
                        out[pl.ds(p*64 + 4*xp + 2*yh2 + s, 8, stride=8), :] = jnp.where(gpar, e, o)
            for i, (xp, yp) in enumerate(par):
                sp = tents[xp, yp] * (v[i] + v[4+i])
                for yh in range(8):
                    rr = jnp.where(inwin, rot(sp, lax.rem(lo - 16*yh + 128, 128)), 0.0)
                    corr[tile, oy + 2*yh + yp, pl.ds(ox + xp, 8, stride=2), :] += rr
        return c
    ng = (live + PAIR - 1) // PAIR
    lax.fori_loop(0, ng, body, 0)
    def zero(p, c):
        out[pl.ds(p*64, 64), :] = jnp.zeros((64, 128), jnp.float32)
        return c
    lax.fori_loop(ng*PAIR, NP, zero, 0)

def prolong(live, off, coef, basis):
    return pl.pallas_call(prolong_kernel, out_shape=jax.ShapeDtypeStruct((2,40,40,128), jnp.float32),
        in_specs=[SM, SM, SM, ANY], out_specs=VM,
        scratch_shapes=[pltpu.VMEM((NP*256,128), jnp.float32), pltpu.SemaphoreType.DMA((NP,))],
        name="prolong")(live, off, coef, basis)

def enrich(live, off, R, K, W):
    return pl.pallas_call(enrich_kernel,
        out_shape=(jax.ShapeDtypeStruct((NP*64,128), jnp.float32), jax.ShapeDtypeStruct((2,40,40,128), jnp.float32)),
        in_specs=[SM, SM, VM, VM, VM], out_specs=(VM, VM),
        scratch_shapes=[pltpu.VMEM((PAIR,192,128), jnp.float32), pltpu.VMEM((PAIR,64,128), jnp.float32), pltpu.VMEM((8,128), jnp.float32)],
        name="enrich")(live, off, R, K, W)

def basis_rows(rb):
    return rb.reshape(NP,NB,32,128).transpose(0,2,1,3).reshape(NP*256,128)
def out_basis(o):
    return o.reshape(NP,32,2,128).transpose(0,2,1,3).reshape(1,1,1,NP,2,4096)
def extended(array, sides, width):
    for axis, dim in sides:
        count, length = (lax.axis_size(axis), array.shape[dim])
        up = [(i, (i + 1) % count) for i in range(count - 1)]
        down = [(j, i) for i, j in up]
        last = lax.slice_in_dim(array, length - width, length, axis=dim)
        leading = lax.slice_in_dim(array, 0, width, axis=dim)
        before = lax.ppermute(last, axis, up)
        after = lax.ppermute(leading, axis, down)
        array = jnp.concatenate([before, array, after], axis=dim)
    return array


def lookup(labels, values):
    accumulated = jnp.zeros(labels.shape, values.dtype)
    for channel in range(values.shape[0]):
        accumulated = accumulated + jnp.where(labels == channel, values[channel], 0.0)
    return accumulated


def neighbour(array, axis_number, offset_step):
    selection = [slice(1, -1), slice(1, -1), slice(1, -1)]
    extent = array.shape[axis_number]
    selection[axis_number] = slice(1 + offset_step, extent - 1 + offset_step)
    return array[tuple(selection)]


def apply_operator(values, conductivity, inside):
    centre = values[1:-1, 1:-1, 1:-1]
    centre_kappa = conductivity[1:-1, 1:-1, 1:-1]
    accumulated = jnp.zeros_like(centre)
    for axis_number in range(3):
        for offset_step in (-1, 1):
            beside_values = neighbour(values, axis_number, offset_step)
            beside_kappa = neighbour(conductivity, axis_number, offset_step)
            beside_inside = neighbour(inside, axis_number, offset_step)
            face_value = jnp.where(
                beside_inside > 0, 0.5 * (centre_kappa + beside_kappa), centre_kappa
            )
            accumulated = accumulated + face_value * (centre - beside_values)
    return accumulated


def axis_mask(position, extent, depth, whole_extent):
    cells = position * extent - depth + jnp.arange(extent + 2 * depth)
    return ((cells >= 0) & (cells < whole_extent)).astype(jnp.float32)


def domain_mask(depth):
    along_x = axis_mask(lax.axis_index("gx"), BX, depth, BX * lax.axis_size("gx"))
    along_y = axis_mask(lax.axis_index("gy"), BY, depth, BY * lax.axis_size("gy"))
    along_z = axis_mask(lax.axis_index("gz"), BZ, depth, BZ * lax.axis_size("gz"))
    return along_x[:, None, None] * along_y[None, :, None] * along_z[None, None, :]


def fold_margins(field_with_halo):
    halo_width = MARGIN
    holder_array = jnp.concatenate([field_with_halo[:halo_width], field_with_halo[-halo_width:]], 0)
    widened_region = extended(holder_array, (("gx", 0),), halo_width)
    inner_region = field_with_halo[halo_width:-halo_width]
    inner_region = (
        inner_region.at[:halo_width]
        .add(widened_region[:halo_width])
        .at[-halo_width:]
        .add(widened_region[-halo_width:])
    )
    holder_array = jnp.concatenate([inner_region[:, :halo_width], inner_region[:, -halo_width:]], 1)
    widened_region = extended(holder_array, (("gy", 1),), halo_width)
    central_part = inner_region[:, halo_width:-halo_width]
    central_part = (
        central_part.at[:, :halo_width]
        .add(widened_region[:, :halo_width])
        .at[:, -halo_width:]
        .add(widened_region[:, -halo_width:])
    )
    holder_array = jnp.concatenate(
        [central_part[:, :, :halo_width], central_part[:, :, -halo_width:]], 2
    )
    widened_region = extended(holder_array, (("gz", 2),), halo_width)
    inner = central_part[:, :, halo_width:-halo_width]
    inner = (
        inner.at[:, :, :halo_width]
        .add(widened_region[:, :, :halo_width])
        .at[:, :, -halo_width:]
        .add(widened_region[:, :, -halo_width:])
    )
    return inner


def tiles(f):
    t = f.transpose(1, 0, 2)
    return jnp.stack([t[:, :, :128], t[:, :, 8:]])


def untile(t):
    s = jnp.pad(t[0], ((0, 0), (0, 0), (0, 8))) + jnp.pad(t[1], ((0, 0), (0, 0), (8, 0)))
    return s.transpose(1, 0, 2)


def local(forcing, kappa_base, labels, contrast, channel_weight, coarse_coef, source_link, offsets, live_pieces, resident_bases):
    kappa = kappa_base * lookup(labels, contrast)
    weight = lookup(labels, channel_weight)
    link_table = source_link[0, 0, 0]
    everything = lax.all_gather(coarse_coef.reshape(1, ND, NB), ("gx", "gy", "gz"), axis=0, tiled=True)
    source_number = (
        (lax.axis_index("gx") + link_table[:, 0] - 1) * lax.axis_size("gy") + lax.axis_index("gy") + link_table[:, 1] - 1
    ) * lax.axis_size("gz") + lax.axis_index("gz") + link_table[:, 2] - 1
    coef_rows = everything[source_number, link_table[:, 3]]
    live = live_pieces.reshape(1)
    off = offsets[0, 0, 0]
    partial_field = untile(prolong(live, off, coef_rows, basis_rows(resident_bases)))
    coarse_field = fold_margins(partial_field)
    axes = (("gx", 0), ("gy", 1), ("gz", 2))
    field_ext, kappa_ext = extended(coarse_field, axes, 1), extended(kappa, axes, 1)
    residual = forcing - apply_operator(field_ext, kappa_ext, domain_mask(1))
    residual_pad, kappa_pad, weight_pad = (extended(f, axes, MARGIN) for f in (residual, kappa, weight))
    out, corr = enrich(live, off, tiles(residual_pad), tiles(kappa_pad), tiles(weight_pad))
    update = coarse_field + fold_margins(untile(corr))
    return update, out_basis(out)


def solution(mesh):
    return jax.shard_map(
        local,
        mesh=mesh,
        in_specs=(
            P("gx", "gy", "gz"),
            P("gx", "gy", "gz"),
            P("gx", "gy", "gz"),
            P(),
            P(),
            P("gx", "gy", "gz", None, None),
            P("gx", "gy", "gz", None, None),
            P("gx", "gy", "gz", None, None),
            P("gx", "gy", "gz"),
            P("gx", "gy", "gz", None, None, None),
        ),
        out_specs=(P("gx", "gy", "gz"), P("gx", "gy", "gz", None, None, None)),
        check_vma=False,
    )
```

time: 1940 us -> 671 us (0.35)
  the two profiles are of different devices: /device:TPU:69 before, /device:TPU:41 now
where the time goes in v1:
time: 671 us; the launch traced here: 670 us
  blocking collectives  271 us (40%)
  starting transfers between devices  191 us (28%)
  local copies, waits for them, and re-layouts  79.3 us (12%)
  waiting for transfers between devices  69.1 us (10%)
  other arithmetic  36 us (5%)
  Pallas kernels  20.8 us (3%)
    all_gather x1, blocking collectives, local(): lax.all_gather(coarse_coef.reshape(1, ND, NB), ('gx', 'gy', 'gz'), axis=0...  271 us
    ppermute x21, starting transfers between devices, extended(): after = lax.ppermute(leading, axis, down)  120 us
    ppermute x21, starting transfers between devices, extended(): before = lax.ppermute(last, axis, up)  70.7 us
    ppermute x21, waiting for transfers between devices, extended(): after = lax.ppermute(leading, axis, down)  47.7 us
    ppermute x21, waiting for transfers between devices, extended(): before = lax.ppermute(last, axis, up)  21.4 us
    scatter-add x4, local copies, waits for them, and re-layouts, fold_margins(): inner = inner.at[:, :, :halo_width].add(widened_region[:, :, :halo_width]...  16.7 us
    pallas_call x1, Pallas kernels, enrich(): pl.pallas_call(enrich_kernel, out_shape=(jax.ShapeDtypeStruct((NP * 64, 1...  16 us
    slice x15, local copies, waits for them, and re-layouts, extended(): last = lax.slice_in_dim(array, length - width, length, axis=dim)  14.1 us
  transfers between devices with their start and end apart: 42, of which 10 were waited for; matrix products, arithmetic and copies ran while one was open for 12% of the time, Pallas kernels for 0%

profile of v1, /device:TPU:41, one launch (start us, length us, event | category | flops | bytes accessed | tf_op | source)
XLA Modules:
  0.0 669.6 jit_solution(570567047595177906)
XLA Ops:
  2.7 271.0 %all-gather = f32[128,1,1,64,8]{3,4,2,1,0:T(8,128)S(1)} all-gather(f32[1,1,1,64,8]{3,4,2,1,0:T(8,128)} %param.39), channel_id=2, replica_groups=mesh['gx'=4,'gy'=4,'gz'=8] {'gx','gy','gz'}, dimensions={0}, use_global_device_ids=true | all-gather | bytes 264192 | tf_op jit(solution)/shard_map/all_gather | solution.py:290
  273.7 2.7 copy.23
  276.4 2.9 gather_fusion
  279.3 4.9 prolong.1
  287.0 4.6 collective-permute-start
  292.9 3.1 select_add_fusion
  296.0 2.9 copy_multiply_fusion
  299.0 34.4 %collective-permute-start.8 = (f32[1,32,128]{2,0,1:T(1,128)S(1)}, f32[1,32,128]{2,0,1:T(1,128)S(1)}, u32[]{:S(2)}, u32[]{:S(2)}) collective-permute-start(f32[1,32,128]{2,0,1:T(1,128)S(1)} %get-tuple-element.208), channel_id=1, source_target_pairs={{32,0},{64,32},{96,64},{33,1},{65,33},{97,65},{34,2},{66,34},{98,6... | collective-permute-start | bytes 49160 | tf_op jit(solution)/shard_map/ppermute | solution.py:195
  335.4 3.4 collective-permute-start.25
  338.7 1.9 collective-permute-start.24
  340.8 15.3 %collective-permute-start.12 = (f32[34,1,128]{2,0,1:T(8,128)S(1)}, f32[34,1,128]{2,0,1:T(8,128)S(1)}, u32[]{:S(2)}, u32[]{:S(2)}) collective-permute-start(f32[34,1,128]{2,0,1:T(8,128)S(1)} %get-tuple-element.198), channel_id=1, source_target_pairs={{8,0},{16,8},{24,16},{9,1},{17,9},{25,17},{10,2},{18,10},{26,18},{... | collective-permute-start | bytes 52232 | tf_op jit(solution)/shard_map/ppermute | solution.py:195
  356.1 1.9 collective-permute-start.10
  361.8 2.4 collective-permute-start.16
  364.5 4.3 collective-permute-start.14
  368.9 2.7 slice.674
  371.6 3.6 collective-permute-start.1
  379.7 3.5 collective-permute-start.30
  383.3 3.5 collective-permute-start.27
  386.8 3.8 collective-permute-start.26
  393.2 3.6 collective-permute-start.32
  399.0 1.9 collective-permute-start.2
  401.0 3.0 collective-permute-start.3
  406.2 2.1 copy.44
  408.3 6.2 collective-permute-start.29
  414.6 2.1 copy.43
  416.7 2.0 collective-permute-start.28
  425.7 5.8 collective-permute-start.5
  431.5 8.3 %collective-permute-done.4 = f32[32,32,4]{2,0,1:T(8,128)S(1)} collective-permute-done((f32[32,32,4]{2,0,1:T(8,128)S(1)}, f32[32,32,4]{2,0,1:T(8,128)S(1)}, u32[]{:S(2)}, u32[]{:S(2)}) %collective-permute-start.4) | collective-permute-done | bytes 16416 | tf_op jit(solution)/shard_map/ppermute | solution.py:194
  440.7 2.7 scatter-add.46
  443.5 3.9 collective-permute-done.5
  447.4 2.0 slice_add_fusion.2
  449.5 6.7 scatter-add.49
  458.7 3.4 collective-permute-start.7
  463.5 2.1 copy.48
  465.6 5.4 collective-permute-start.35
  471.0 2.2 copy.47
  473.2 2.1 collective-permute-start.34
  476.6 2.1 copy.45
  479.4 3.4 collective-permute-start.13
  482.8 2.2 collective-permute-start.11
  485.0 3.1 maximum_bitcast_fusion.1
  490.1 2.0 copy.36
  492.1 5.8 collective-permute-start.17
  500.7 3.1 slice_bitcast_fusion.3
  503.9 2.2 copy.50
  506.1 2.1 copy.49
  508.2 2.0 copy.37
  511.5 5.6 fusion.3
  517.1 2.5 collective-permute-start.19
  519.6 2.8 collective-permute-start.18
  524.6 3.9 collective-permute-start.21
  535.0 6.0 collective-permute-start.23
  544.4 3.6 pad_maximum_fusion.1
  551.3 2.0 maximum_bitcast_fusion
  554.9 16.0 %enrich.1 = (f32[2560,128]{1,0:T(8,128)}, f32[2,40,40,128]{3,2,1,0:T(8,128)}) custom-call(s32[1]{0:T(128)} %bitcast.55.live_ref, s32[40,3]{1,0:T(8,128)} %bitcast.59, f32[2,40,40,128]{3,2,1,0:T(8,128)} %pad_maximum_fusion.R, f32[2,40,40,128]{3,2,1,0:T(8,128)} %get-tuple-element.221.K, f32[2,40,40,128]{3,2,1,0:T(8,128)} %get-tuple-element.222.W), custom_call_target="tpu_custom_call" | custom-call | tf_op jit(solution)/shard_map/enrich/pallas_call | solution.py:177
  572.9 14.7 %collective-permute-start.36 = (f32[4,40,136]{2,0,1:T(4,128)S(1)}, f32[4,40,136]{2,0,1:T(4,128)S(1)}, u32[]{:S(2)}, u32[]{:S(2)}) collective-permute-start(f32[4,40,136]{2,0,1:T(4,128)S(1)} %get-tuple-element.160), channel_id=1, source_target_pairs={{0,32},{32,64},{64,96},{1,33},{33,65},{65,97},{2,34},{34,66},{66,9... | collective-permute-start | bytes 261128 | tf_op jit(solution)/shard_map/ppermute | solution.py:194
  590.0 9.8 %collective-permute-done.37 = f32[4,40,136]{2,0,1:T(4,128)S(1)} collective-permute-done((f32[4,40,136]{2,0,1:T(4,128)S(1)}, f32[4,40,136]{2,0,1:T(4,128)S(1)}, u32[]{:S(2)}, u32[]{:S(2)}) %collective-permute-start.37) | collective-permute-done | bytes 87072 | tf_op jit(solution)/shard_map/ppermute | solution.py:195
  599.8 6.5 collective-permute-start.38
  606.4 2.1 collective-permute-start.39
  608.6 4.3 collective-permute-done.39
  615.2 5.8 collective-permute-start.41
  621.0 10.0 %collective-permute-done.40 = f32[32,32,4]{2,0,1:T(8,128)S(1)} collective-permute-done((f32[32,32,4]{2,0,1:T(8,128)S(1)}, f32[32,32,4]{2,0,1:T(8,128)S(1)}, u32[]{:S(2)}, u32[]{:S(2)}) %collective-permute-start.40) | collective-permute-done | bytes 16416 | tf_op jit(solution)/shard_map/ppermute | solution.py:194
  632.7 29.7 %collective-permute-done.41 = f32[32,32,4]{2,0,1:T(8,128)S(1)} collective-permute-done((f32[32,32,4]{2,0,1:T(8,128)S(1)}, f32[32,32,4]{2,0,1:T(8,128)S(1)}, u32[]{:S(2)}, u32[]{:S(2)}) %collective-permute-start.41) | collective-permute-done | bytes 16416 | tf_op jit(solution)/shard_map/ppermute | solution.py:195
  662.5 5.9 scatter-add.59
  (192 shorter events, 69.7 us)
Async XLA Ops:
  286.2 12.7 %copy-start.3 = (f32[40,40,136]{2,0,1:T(8,128)}, f32[40,40,136]{2,0,1:T(8,128)S(1)}, u32[]{:S(2)}) copy-start(f32[40,40,136]{2,0,1:T(8,128)S(1)} %add_bitcast_fusion.1) | copy-start | bytes 2611204
  286.3 9.8 %copy-start.20 = (f32[32,32,128]{2,1,0:T(8,128)S(1)}, f32[32,32,128]{2,1,0:T(8,128)}, u32[]{:S(2)}) copy-start(f32[32,32,128]{2,1,0:T(8,128)} %param.35) | copy-start | bytes 1572868
  287.0 106.2 %collective-permute-start = (f32[4,40,136]{2,0,1:T(4,128)}, f32[4,40,136]{2,0,1:T(4,128)}, u32[]{:S(2)}, u32[]{:S(2)}) collective-permute-start(f32[4,40,136]{2,0,1:T(4,128)} %get-tuple-element.170), channel_id=1, source_target_pairs={{0,32},{32,64},{64,96},{1,33},{33,65},{65,97},{2,34},{34,66},{66,9... | collective-permute-start | bytes 261128 | tf_op jit(solution)/shard_map/ppermute | solution.py:194
  296.0 127.5 %copy-start = (f32[32,32,128]{2,0,1:T(8,128)}, f32[32,32,128]{2,0,1:T(8,128)S(1)}, u32[]{:S(2)}) copy-start(f32[32,32,128]{2,0,1:T(8,128)S(1)} %get-tuple-element.154) | copy-start | bytes 1572868
  299.0 41.8 %collective-permute-start.8 = (f32[1,32,128]{2,0,1:T(1,128)S(1)}, f32[1,32,128]{2,0,1:T(1,128)S(1)}, u32[]{:S(2)}, u32[]{:S(2)}) collective-permute-start(f32[1,32,128]{2,0,1:T(1,128)S(1)} %get-tuple-element.208), channel_id=1, source_target_pairs={{32,0},{64,32},{96,64},{33,1},{65,33},{97,65},{34,2},{66,34},{98,6... | collective-permute-start | bytes 49160 | tf_op jit(solution)/shard_map/ppermute | solution.py:195
  333.4 7.4 %collective-permute-start.6 = (f32[1,32,128]{2,0,1:T(1,128)S(1)}, f32[1,32,128]{2,0,1:T(1,128)S(1)}, u32[]{:S(2)}, u32[]{:S(2)}) collective-permute-start(f32[1,32,128]{2,0,1:T(1,128)S(1)} %get-tuple-element.207), channel_id=1, source_target_pairs={{0,32},{32,64},{64,96},{1,33},{33,65},{65,97},{2,34},{34,66},{66,9... | collective-permute-start | bytes 49160 | tf_op jit(solution)/shard_map/ppermute | solution.py:194
  335.4 44.4 %collective-permute-start.25 = (f32[4,32,128]{2,0,1:T(4,128)S(1)}, f32[4,32,128]{2,0,1:T(4,128)S(1)}, u32[]{:S(2)}, u32[]{:S(2)}) collective-permute-start(f32[4,32,128]{2,0,1:T(4,128)S(1)} %get-tuple-element.204), channel_id=1, source_target_pairs={{32,0},{64,32},{96,64},{33,1},{65,33},{97,65},{34,2},{66,34},{98,6... | collective-permute-start | bytes 196616 | tf_op jit(solution)/shard_map/ppermute | solution.py:195
  338.7 44.5 %collective-permute-start.24 = (f32[4,32,128]{2,0,1:T(4,128)S(1)}, f32[4,32,128]{2,0,1:T(4,128)S(1)}, u32[]{:S(2)}, u32[]{:S(2)}) collective-permute-start(f32[4,32,128]{2,0,1:T(4,128)S(1)} %get-tuple-element.203), channel_id=1, source_target_pairs={{0,32},{32,64},{64,96},{1,33},{33,65},{65,97},{2,34},{34,66},{66,9... | collective-permute-start | bytes 196616 | tf_op jit(solution)/shard_map/ppermute | solution.py:194
  340.8 18.5 %copy-start.25 = (f32[1,32,128]{2,0,1:T(1,128)}, f32[1,32,128]{2,0,1:T(1,128)S(1)}, u32[]{:S(2)}) copy-start(f32[1,32,128]{2,0,1:T(1,128)S(1)} %collective-permute-done.8) | copy-start | bytes 49156
  340.8 18.5 %copy-start.27 = (f32[1,32,128]{2,0,1:T(1,128)}, f32[1,32,128]{2,0,1:T(1,128)S(1)}, u32[]{:S(2)}) copy-start(f32[1,32,128]{2,0,1:T(1,128)S(1)} %collective-permute-done.6) | copy-start | bytes 49156
  340.8 17.4 %collective-permute-start.12 = (f32[34,1,128]{2,0,1:T(8,128)S(1)}, f32[34,1,128]{2,0,1:T(8,128)S(1)}, u32[]{:S(2)}, u32[]{:S(2)}) collective-permute-start(f32[34,1,128]{2,0,1:T(8,128)S(1)} %get-tuple-element.198), channel_id=1, source_target_pairs={{8,0},{16,8},{24,16},{9,1},{17,9},{25,17},{10,2},{18,10},{26,18},{... | collective-permute-start | bytes 52232 | tf_op jit(solution)/shard_map/ppermute | solution.py:195
  356.1 3.1 collective-permute-start.10
  361.8 9.8 %collective-permute-start.16 = (f32[34,34,1]{1,2,0:T(1,128)S(1)}, f32[34,34,1]{1,2,0:T(1,128)S(1)}, u32[]{:S(2)}, u32[]{:S(2)}) collective-permute-start(f32[34,34,1]{1,2,0:T(1,128)S(1)} %copy.34), channel_id=1, source_target_pairs={{1,0},{2,1},{3,2},{4,3},{5,4},{6,5},{7,6},{9,8},{10,9},{11,10},{12... | collective-permute-start | bytes 13880 | tf_op jit(solution)/shard_map/ppermute | solution.py:195
  364.5 12.0 %collective-permute-start.14 = (f32[34,34,1]{1,2,0:T(1,128)S(1)}, f32[34,34,1]{1,2,0:T(1,128)S(1)}, u32[]{:S(2)}, u32[]{:S(2)}) collective-permute-start(f32[34,34,1]{1,2,0:T(1,128)S(1)} %copy.30), channel_id=1, source_target_pairs={{0,1},{1,2},{2,3},{3,4},{4,5},{5,6},{6,7},{8,9},{9,10},{10,11},{11... | collective-permute-start | bytes 13880 | tf_op jit(solution)/shard_map/ppermute | solution.py:194
  371.6 26.4 %collective-permute-start.1 = (f32[4,40,136]{2,0,1:T(4,128)}, f32[4,40,136]{2,0,1:T(4,128)S(1)}, u32[]{:S(2)}, u32[]{:S(2)}) collective-permute-start(f32[4,40,136]{2,0,1:T(4,128)} %get-tuple-element.169), channel_id=1, source_target_pairs={{32,0},{64,32},{96,64},{33,1},{65,33},{97,65},{34,2},{66,34},{98,6... | collective-permute-start | bytes 261128 | tf_op jit(solution)/shard_map/ppermute | solution.py:195
  376.5 10.2 %collective-permute-start.31 = (f32[4,32,128]{2,0,1:T(4,128)S(1)}, f32[4,32,128]{2,0,1:T(4,128)S(1)}, u32[]{:S(2)}, u32[]{:S(2)}) collective-permute-start(f32[4,32,128]{2,0,1:T(4,128)S(1)} %get-tuple-element.202), channel_id=1, source_target_pairs={{32,0},{64,32},{96,64},{33,1},{65,33},{97,65},{34,2},{66,34},{98,6... | collective-permute-start | bytes 196616 | tf_op jit(solution)/shard_map/ppermute | solution.py:195
  379.7 17.1 %copy-start.4 = (f32[32,40,136]{2,0,1:T(8,128)S(1)}, f32[32,40,136]{2,0,1:T(8,128)}, u32[]{:S(2)}) copy-start(f32[32,40,136]{2,0,1:T(8,128)} %slice.674) | copy-start | bytes 2088964
  379.7 10.8 %collective-permute-start.30 = (f32[4,32,128]{2,0,1:T(4,128)S(1)}, f32[4,32,128]{2,0,1:T(4,128)S(1)}, u32[]{:S(2)}, u32[]{:S(2)}) collective-permute-start(f32[4,32,128]{2,0,1:T(4,128)S(1)} %get-tuple-element.201), channel_id=1, source_target_pairs={{0,32},{32,64},{64,96},{1,33},{33,65},{65,97},{2,34},{34,66},{66,9... | collective-permute-start | bytes 196616 | tf_op jit(solution)/shard_map/ppermute | solution.py:194
  383.2 14.9 %copy-start.9 = (f32[4,32,128]{2,0,1:T(4,128)}, f32[4,32,128]{2,0,1:T(4,128)S(1)}, u32[]{:S(2)}) copy-start(f32[4,32,128]{2,0,1:T(4,128)S(1)} %collective-permute-done.24) | copy-start | bytes 196612
  383.3 17.7 %collective-permute-start.27 = (f32[40,4,128]{2,0,1:T(8,128)S(1)}, f32[40,4,128]{2,0,1:T(8,128)S(1)}, u32[]{:S(2)}, u32[]{:S(2)}) collective-permute-start(f32[40,4,128]{2,0,1:T(8,128)S(1)} %get-tuple-element.194), channel_id=1, source_target_pairs={{8,0},{16,8},{24,16},{9,1},{17,9},{25,17},{10,2},{18,10},{26,18},{... | collective-permute-start | bytes 245768 | tf_op jit(solution)/shard_map/ppermute | solution.py:195
  386.8 11.4 %copy-start.12 = (f32[4,32,128]{2,0,1:T(4,128)}, f32[4,32,128]{2,0,1:T(4,128)S(1)}, u32[]{:S(2)}) copy-start(f32[4,32,128]{2,0,1:T(4,128)S(1)} %collective-permute-done.31) | copy-start | bytes 196612
  386.8 17.3 %collective-permute-start.26 = (f32[40,4,128]{2,0,1:T(8,128)S(1)}, f32[40,4,128]{2,0,1:T(8,128)S(1)}, u32[]{:S(2)}, u32[]{:S(2)}) collective-permute-start(f32[40,4,128]{2,0,1:T(8,128)S(1)} %get-tuple-element.193), channel_id=1, source_target_pairs={{0,8},{8,16},{16,24},{1,9},{9,17},{17,25},{2,10},{10,18},{18,26},{... | collective-permute-start | bytes 245768 | tf_op jit(solution)/shard_map/ppermute | solution.py:194
  391.3 32.3 %collective-permute-start.33 = (f32[40,4,128]{2,0,1:T(8,128)}, f32[40,4,128]{2,0,1:T(8,128)}, u32[]{:S(2)}, u32[]{:S(2)}) collective-permute-start(f32[40,4,128]{2,0,1:T(8,128)} %get-tuple-element.192), channel_id=1, source_target_pairs={{8,0},{16,8},{24,16},{9,1},{17,9},{25,17},{10,2},{18,10},{26,18},{... | collective-permute-start | bytes 245768 | tf_op jit(solution)/shard_map/ppermute | solution.py:195
  393.2 30.3 %collective-permute-start.32 = (f32[40,4,128]{2,0,1:T(8,128)}, f32[40,4,128]{2,0,1:T(8,128)}, u32[]{:S(2)}, u32[]{:S(2)}) collective-permute-start(f32[40,4,128]{2,0,1:T(8,128)} %get-tuple-element.191), channel_id=1, source_target_pairs={{0,8},{8,16},{16,24},{1,9},{9,17},{17,25},{2,10},{10,18},{18,26},{... | collective-permute-start | bytes 245768 | tf_op jit(solution)/shard_map/ppermute | solution.py:194
  399.0 17.6 %collective-permute-start.2 = (f32[32,4,136]{2,0,1:T(8,128)}, f32[32,4,136]{2,0,1:T(8,128)}, u32[]{:S(2)}, u32[]{:S(2)}) collective-permute-start(f32[32,4,136]{2,0,1:T(8,128)} %get-tuple-element.176), channel_id=1, source_target_pairs={{0,8},{8,16},{16,24},{1,9},{9,17},{17,25},{2,10},{10,18},{18,26},{... | collective-permute-start | bytes 208904 | tf_op jit(solution)/shard_map/ppermute | solution.py:194
  401.0 18.7 %collective-permute-start.3 = (f32[32,4,136]{2,0,1:T(8,128)}, f32[32,4,136]{2,0,1:T(8,128)}, u32[]{:S(2)}, u32[]{:S(2)}) collective-permute-start(f32[32,4,136]{2,0,1:T(8,128)} %get-tuple-element.175), channel_id=1, source_target_pairs={{8,0},{16,8},{24,16},{9,1},{17,9},{25,17},{10,2},{18,10},{26,18},{... | collective-permute-start | bytes 208904 | tf_op jit(solution)/shard_map/ppermute | solution.py:195
  408.3 64.9 %collective-permute-start.29 = (f32[40,40,4]{1,0,2:T(8,128)}, f32[40,40,4]{1,0,2:T(8,128)}, u32[]{:S(2)}, u32[]{:S(2)}) collective-permute-start(f32[40,40,4]{1,0,2:T(8,128)} %copy.44), channel_id=1, source_target_pairs={{1,0},{2,1},{3,2},{4,3},{5,4},{6,5},{7,6},{9,8},{10,9},{11,10},{12... | collective-permute-start | bytes 76808 | tf_op jit(solution)/shard_map/ppermute | solution.py:195
  416.7 59.9 %collective-permute-start.28 = (f32[40,40,4]{1,0,2:T(8,128)}, f32[40,40,4]{1,0,2:T(8,128)}, u32[]{:S(2)}, u32[]{:S(2)}) collective-permute-start(f32[40,40,4]{1,0,2:T(8,128)} %copy.43), channel_id=1, source_target_pairs={{0,1},{1,2},{2,3},{3,4},{4,5},{5,6},{6,7},{8,9},{9,10},{10,11},{11... | collective-permute-start | bytes 76808 | tf_op jit(solution)/shard_map/ppermute | solution.py:194
  421.6 18.1 %collective-permute-start.4 = (f32[32,32,4]{2,0,1:T(8,128)S(1)}, f32[32,32,4]{2,0,1:T(8,128)S(1)}, u32[]{:S(2)}, u32[]{:S(2)}) collective-permute-start(f32[32,32,4]{2,0,1:T(8,128)S(1)} %get-tuple-element.180), channel_id=1, source_target_pairs={{0,1},{1,2},{2,3},{3,4},{4,5},{5,6},{6,7},{8,9},{9,10},{10,11},{11... | collective-permute-start | bytes 49160 | tf_op jit(solution)/shard_map/ppermute | solution.py:194
  425.7 21.7 %collective-permute-start.5 = (f32[32,32,4]{2,0,1:T(8,128)}, f32[32,32,4]{2,0,1:T(8,128)}, u32[]{:S(2)}, u32[]{:S(2)}) collective-permute-start(f32[32,32,4]{2,0,1:T(8,128)} %get-tuple-element.179), channel_id=1, source_target_pairs={{1,0},{2,1},{3,2},{4,3},{5,4},{6,5},{7,6},{9,8},{10,9},{11,10},{12... | collective-permute-start | bytes 49160 | tf_op jit(solution)/shard_map/ppermute | solution.py:195
  440.7 21.3 %copy-start.2 = (f32[40,40,128]{2,0,1:T(8,128)S(1)}, f32[40,40,128]{2,0,1:T(8,128)}, u32[]{:S(2)}) copy-start(f32[40,40,128]{2,0,1:T(8,128)} %pad_maximum_fusion.5) | copy-start | bytes 2457604
  456.8 21.9 %collective-permute-start.9 = (f32[1,32,128]{2,0,1:T(1,128)}, f32[1,32,128]{2,0,1:T(1,128)}, u32[]{:S(2)}, u32[]{:S(2)}) collective-permute-start(f32[1,32,128]{2,0,1:T(1,128)} %get-tuple-element.210), channel_id=1, source_target_pairs={{32,0},{64,32},{96,64},{33,1},{65,33},{97,65},{34,2},{66,34},{98,6... | collective-permute-start | bytes 49160 | tf_op jit(solution)/shard_map/ppermute | solution.py:195
  458.7 20.0 %collective-permute-start.7 = (f32[1,32,128]{2,0,1:T(1,128)}, f32[1,32,128]{2,0,1:T(1,128)}, u32[]{:S(2)}, u32[]{:S(2)}) collective-permute-start(f32[1,32,128]{2,0,1:T(1,128)} %get-tuple-element.209), channel_id=1, source_target_pairs={{0,32},{32,64},{64,96},{1,33},{33,65},{65,97},{2,34},{34,66},{66,9... | collective-permute-start | bytes 49160 | tf_op jit(solution)/shard_map/ppermute | solution.py:194
  465.6 38.3 %collective-permute-start.35 = (f32[40,40,4]{1,0,2:T(8,128)}, f32[40,40,4]{1,0,2:T(8,128)}, u32[]{:S(2)}, u32[]{:S(2)}) collective-permute-start(f32[40,40,4]{1,0,2:T(8,128)} %copy.48), channel_id=1, source_target_pairs={{1,0},{2,1},{3,2},{4,3},{5,4},{6,5},{7,6},{9,8},{10,9},{11,10},{12... | collective-permute-start | bytes 76808 | tf_op jit(solution)/shard_map/ppermute | solution.py:195
  471.0 14.0 %copy-start.11 = (f32[4,32,128]{2,0,1:T(4,128)S(1)}, f32[4,32,128]{2,0,1:T(4,128)}, u32[]{:S(2)}) copy-start(f32[4,32,128]{2,0,1:T(4,128)} %copy-done.9) | copy-start | bytes 196612
  471.0 14.0 %copy-start.22 = (f32[40,4,128]{2,0,1:T(8,128)S(1)}, f32[40,4,128]{2,0,1:T(8,128)}, u32[]{:S(2)}) copy-start(f32[40,4,128]{2,0,1:T(8,128)} %copy-done.21) | copy-start | bytes 245764
  471.0 14.0 %copy-start.24 = (f32[40,4,128]{2,0,1:T(8,128)S(1)}, f32[40,4,128]{2,0,1:T(8,128)}, u32[]{:S(2)}) copy-start(f32[40,4,128]{2,0,1:T(8,128)} %copy-done.23) | copy-start | bytes 245764
  473.2 32.9 %collective-permute-start.34 = (f32[40,40,4]{1,0,2:T(8,128)}, f32[40,40,4]{1,0,2:T(8,128)}, u32[]{:S(2)}, u32[]{:S(2)}) collective-permute-start(f32[40,40,4]{1,0,2:T(8,128)} %copy.47), channel_id=1, source_target_pairs={{0,1},{1,2},{2,3},{3,4},{4,5},{5,6},{6,7},{8,9},{9,10},{10,11},{11... | collective-permute-start | bytes 76808 | tf_op jit(solution)/shard_map/ppermute | solution.py:194
  479.4 8.8 %collective-permute-start.13 = (f32[34,1,128]{2,0,1:T(8,128)S(1)}, f32[34,1,128]{2,0,1:T(8,128)S(1)}, u32[]{:S(2)}, u32[]{:S(2)}) collective-permute-start(f32[34,1,128]{2,0,1:T(8,128)S(1)} %get-tuple-element.200), channel_id=1, source_target_pairs={{8,0},{16,8},{24,16},{9,1},{17,9},{25,17},{10,2},{18,10},{26,18},{... | collective-permute-start | bytes 52232 | tf_op jit(solution)/shard_map/ppermute | solution.py:195
  482.8 5.4 collective-permute-start.11
  492.1 16.1 %collective-permute-start.17 = (f32[34,34,1]{1,2,0:T(1,128)}, f32[34,34,1]{1,2,0:T(1,128)}, u32[]{:S(2)}, u32[]{:S(2)}) collective-permute-start(f32[34,34,1]{1,2,0:T(1,128)} %copy.36), channel_id=1, source_target_pairs={{1,0},{2,1},{3,2},{4,3},{5,4},{6,5},{7,6},{9,8},{10,9},{11,10},{12... | collective-permute-start | bytes 13880 | tf_op jit(solution)/shard_map/ppermute | solution.py:195
  498.8 11.4 %collective-permute-start.15 = (f32[34,34,1]{1,2,0:T(1,128)}, f32[34,34,1]{1,2,0:T(1,128)S(1)}, u32[]{:S(2)}, u32[]{:S(2)}) collective-permute-start(f32[34,34,1]{1,2,0:T(1,128)} %copy.32), channel_id=1, source_target_pairs={{0,1},{1,2},{2,3},{3,4},{4,5},{5,6},{6,7},{8,9},{9,10},{10,11},{11... | collective-permute-start | bytes 13880 | tf_op jit(solution)/shard_map/ppermute | solution.py:194
  503.9 7.6 %copy-start.18 = (f32[32,32,128]{2,1,0:T(8,128)S(1)}, f32[32,32,128]{2,1,0:T(8,128)}, u32[]{:S(2)}) copy-start(f32[32,32,128]{2,1,0:T(8,128)} %param.34) | copy-start | bytes 1572868
  503.9 7.6 %copy-start.26 = (f32[1,32,128]{2,0,1:T(1,128)S(1)}, f32[1,32,128]{2,0,1:T(1,128)}, u32[]{:S(2)}) copy-start(f32[1,32,128]{2,0,1:T(1,128)} %copy-done.25) | copy-start | bytes 49156
  503.9 7.6 %copy-start.28 = (f32[1,32,128]{2,0,1:T(1,128)S(1)}, f32[1,32,128]{2,0,1:T(1,128)}, u32[]{:S(2)}) copy-start(f32[1,32,128]{2,0,1:T(1,128)} %copy-done.27) | copy-start | bytes 49156
  503.9 7.6 %copy-start.30 = (f32[34,1,128]{2,0,1:T(8,128)S(1)}, f32[34,1,128]{2,0,1:T(8,128)}, u32[]{:S(2)}) copy-start(f32[34,1,128]{2,0,1:T(8,128)} %copy-done.29) | copy-start | bytes 52228
  511.5 11.0 %copy-start.1 = (f32[32,32,128]{2,0,1:T(8,128)S(1)}, f32[32,32,128]{2,0,1:T(8,128)}, u32[]{:S(2)}) copy-start(f32[32,32,128]{2,0,1:T(8,128)} %copy-done) | copy-start | bytes 1572868
  511.5 11.0 %copy-start.7 = (f32[40,40,4]{2,0,1:T(8,128)S(1)}, f32[40,40,4]{2,0,1:T(8,128)}, u32[]{:S(2)}) copy-start(f32[40,40,4]{2,0,1:T(8,128)} %copy.50) | copy-start | bytes 76804
  511.5 11.0 %copy-start.8 = (f32[40,40,4]{2,0,1:T(8,128)S(1)}, f32[40,40,4]{2,0,1:T(8,128)}, u32[]{:S(2)}) copy-start(f32[40,40,4]{2,0,1:T(8,128)} %copy.49) | copy-start | bytes 76804
  511.5 11.0 %copy-start.14 = (f32[4,32,128]{2,0,1:T(4,128)S(1)}, f32[4,32,128]{2,0,1:T(4,128)}, u32[]{:S(2)}) copy-start(f32[4,32,128]{2,0,1:T(4,128)} %copy-done.12) | copy-start | bytes 196612
  511.5 11.0 %copy-start.17 = (f32[4,32,128]{2,0,1:T(4,128)S(1)}, f32[4,32,128]{2,0,1:T(4,128)}, u32[]{:S(2)}) copy-start(f32[4,32,128]{2,0,1:T(4,128)} %copy-done.15) | copy-start | bytes 196612
  517.1 7.1 %collective-permute-start.19 = (f32[4,32,128]{2,0,1:T(4,128)S(1)}, f32[4,32,128]{2,0,1:T(4,128)S(1)}, u32[]{:S(2)}, u32[]{:S(2)}) collective-permute-start(f32[4,32,128]{2,0,1:T(4,128)S(1)} %get-tuple-element.206), channel_id=1, source_target_pairs={{32,0},{64,32},{96,64},{33,1},{65,33},{97,65},{34,2},{66,34},{98,6... | collective-permute-start | bytes 196616 | tf_op jit(solution)/shard_map/ppermute | solution.py:195
  519.6 5.0 collective-permute-start.18
  524.6 7.2 %collective-permute-start.21 = (f32[40,4,128]{2,0,1:T(8,128)S(1)}, f32[40,4,128]{2,0,1:T(8,128)S(1)}, u32[]{:S(2)}, u32[]{:S(2)}) collective-permute-start(f32[40,4,128]{2,0,1:T(8,128)S(1)} %get-tuple-element.196), channel_id=1, source_target_pairs={{8,0},{16,8},{24,16},{9,1},{17,9},{25,17},{10,2},{18,10},{26,18},{... | collective-permute-start | bytes 245768 | tf_op jit(solution)/shard_map/ppermute | solution.py:195
  528.5 3.4 collective-permute-start.20
  533.4 11.0 %copy-start.6 = (f32[1,40,40,128]{3,2,1,0:T(8,128)S(1)}, f32[1,40,40,128]{3,2,1,0:T(8,128)}, u32[]{:S(2)}) copy-start(f32[1,40,40,128]{3,2,1,0:T(8,128)} %get-tuple-element.165) | copy-start | bytes 2457604
  535.0 13.0 %collective-permute-start.23 = (f32[40,40,4]{1,0,2:T(8,128)S(1)}, f32[40,40,4]{1,0,2:T(8,128)S(1)}, u32[]{:S(2)}, u32[]{:S(2)}) collective-permute-start(f32[40,40,4]{1,0,2:T(8,128)S(1)} %copy.40), channel_id=1, source_target_pairs={{1,0},{2,1},{3,2},{4,3},{5,4},{6,5},{7,6},{9,8},{10,9},{11,10},{12... | collective-permute-start | bytes 76808 | tf_op jit(solution)/shard_map/ppermute | solution.py:195
  542.5 7.6 %collective-permute-start.22 = (f32[40,40,4]{1,0,2:T(8,128)S(1)}, f32[40,40,4]{1,0,2:T(8,128)S(1)}, u32[]{:S(2)}, u32[]{:S(2)}) collective-permute-start(f32[40,40,4]{1,0,2:T(8,128)S(1)} %copy.39), channel_id=1, source_target_pairs={{0,1},{1,2},{2,3},{3,4},{4,5},{5,6},{6,7},{8,9},{9,10},{10,11},{11... | collective-permute-start | bytes 76808 | tf_op jit(solution)/shard_map/ppermute | solution.py:194
  572.9 16.9 %collective-permute-start.36 = (f32[4,40,136]{2,0,1:T(4,128)S(1)}, f32[4,40,136]{2,0,1:T(4,128)S(1)}, u32[]{:S(2)}, u32[]{:S(2)}) collective-permute-start(f32[4,40,136]{2,0,1:T(4,128)S(1)} %get-tuple-element.160), channel_id=1, source_target_pairs={{0,32},{32,64},{64,96},{1,33},{33,65},{65,97},{2,34},{34,66},{66,9... | collective-permute-start | bytes 261128 | tf_op jit(solution)/shard_map/ppermute | solution.py:194
  587.8 11.9 %collective-permute-start.37 = (f32[4,40,136]{2,0,1:T(4,128)S(1)}, f32[4,40,136]{2,0,1:T(4,128)S(1)}, u32[]{:S(2)}, u32[]{:S(2)}) collective-permute-start(f32[4,40,136]{2,0,1:T(4,128)S(1)} %get-tuple-element.159), channel_id=1, source_target_pairs={{32,0},{64,32},{96,64},{33,1},{65,33},{97,65},{34,2},{66,34},{98,6... | collective-permute-start | bytes 261128 | tf_op jit(solution)/shard_map/ppermute | solution.py:195
  599.8 8.7 %collective-permute-start.38 = (f32[32,4,136]{2,0,1:T(8,128)S(1)}, f32[32,4,136]{2,0,1:T(8,128)S(1)}, u32[]{:S(2)}, u32[]{:S(2)}) collective-permute-start(f32[32,4,136]{2,0,1:T(8,128)S(1)} %get-tuple-element.174), channel_id=1, source_target_pairs={{0,8},{8,16},{16,24},{1,9},{9,17},{17,25},{2,10},{10,18},{18,26},{... | collective-permute-start | bytes 208904 | tf_op jit(solution)/shard_map/ppermute | solution.py:194
  606.4 6.5 collective-permute-start.39
  613.1 17.9 %collective-permute-start.40 = (f32[32,32,4]{2,0,1:T(8,128)S(1)}, f32[32,32,4]{2,0,1:T(8,128)S(1)}, u32[]{:S(2)}, u32[]{:S(2)}) collective-permute-start(f32[32,32,4]{2,0,1:T(8,128)S(1)} %get-tuple-element.178), channel_id=1, source_target_pairs={{0,1},{1,2},{2,3},{3,4},{4,5},{5,6},{6,7},{8,9},{9,10},{10,11},{11... | collective-permute-start | bytes 49160 | tf_op jit(solution)/shard_map/ppermute | solution.py:194
  615.2 47.1 %collective-permute-start.41 = (f32[32,32,4]{2,0,1:T(8,128)S(1)}, f32[32,32,4]{2,0,1:T(8,128)S(1)}, u32[]{:S(2)}, u32[]{:S(2)}) collective-permute-start(f32[32,32,4]{2,0,1:T(8,128)S(1)} %get-tuple-element.177), channel_id=1, source_target_pairs={{1,0},{2,1},{3,2},{4,3},{5,4},{6,5},{7,6},{9,8},{10,9},{11,10},{12... | collective-permute-start | bytes 49160 | tf_op jit(solution)/shard_map/ppermute | solution.py:195
  (15 other events, 66.0 us)

commit v2 on v1

v2 whole, which is shorter than its diff:
```python
import jax
import jax.numpy as jnp
from jax import lax
from jax.experimental import pallas as pl
from jax.experimental.pallas import tpu as pltpu
from jax.sharding import PartitionSpec as P

ND = 64
PIECE=16; NB=8; NP=40; SWEEPS=20
OMEGA = 2.0/3.0
PAIR = 2
VM = pl.BlockSpec(memory_space=pltpu.VMEM)
SM = pl.BlockSpec(memory_space=pltpu.SMEM)
ANY = pl.BlockSpec(memory_space=pl.ANY)

def corner(off, p):
    ox = jnp.clip(off[p, 0], 0, 24)
    oy = jnp.clip(off[p, 1], 0, 24)
    oz = jnp.clip(off[p, 2], 0, 120)
    tile = (oz > 112).astype(jnp.int32)
    return ox, oy, tile, oz - 8 * tile

def rot(v, shift, axis=1):
    return pltpu.roll(v, shift, axis)

def lanes_sub():
    return lax.broadcasted_iota(jnp.int32, (8, 128), 1), lax.broadcasted_iota(jnp.int32, (8, 128), 0)

MESH = pl.DeviceIdType.MESH
SIZE = {"gx": 4, "gy": 4, "gz": 8}
BIG = 56 * 1024 * 1024


def ring(axis, step):
    n = SIZE[axis]
    return lax.rem(lax.axis_index(axis) + (step + n), n)


def greet(pairs):
    barrier = pltpu.get_barrier_semaphore()
    for axis, step in pairs:
        pl.semaphore_signal(barrier, inc=1, device_id={axis: ring(axis, step)}, device_id_type=MESH)
    pl.semaphore_wait(barrier, len(pairs))


def remote(src, dst, send, recv, i, axis, step):
    copy = pltpu.make_async_remote_copy(
        src_ref=src, dst_ref=dst, send_sem=send.at[i], recv_sem=recv.at[i],
        device_id={axis: ring(axis, step)}, device_id_type=MESH,
    )
    copy.start()
    return copy


def edges(axis):
    i = lax.axis_index(axis)
    return (jnp.where(i > 0, 1.0, 0.0), jnp.where(i < SIZE[axis] - 1, 1.0, 0.0))


def group_row(g, pos):
    return 8 * g - 4 + pos


def share_kernel(coef, forcing, base, labels, con, chw, gat, E, G, zs, zr, yr, yg, xs, xr, xgs, xgr, send, recv):
    ix, iy, iz = lax.axis_index("gx"), lax.axis_index("gy"), lax.axis_index("gz")
    gather = [("gz", s) for s in range(1, 8)] + [("gy", s) for s in range(1, 4)] + [("gx", s) for s in range(1, 4)]
    greet(gather)
    me = (ix * 4 + iy) * 8 + iz
    g1 = [remote(coef.at[0], gat.at[me], send, recv, s - 1, "gz", s) for s in range(1, 8)]
    gat[me] = coef[0]
    lane, sub = lanes_sub()
    E[...] = jnp.zeros_like(E)
    G[...] = jnp.zeros_like(G)

    def fill(y, c):
        for xo in range(4):
            rows = pl.ds(xo * 256 + y, 8, stride=32)
            lab = labels[rows, :]
            kappa = jnp.zeros((8, 128), jnp.float32)
            weight = jnp.zeros((8, 128), jnp.float32)
            for ch in range(4):
                kappa = jnp.where(lab == ch, con[ch], kappa)
                weight = jnp.where(lab == ch, chw[ch], weight)
            E[0, y + 8, pl.ds(8 + 8 * xo, 8), :] = forcing[rows, :]
            E[1, y + 8, pl.ds(8 + 8 * xo, 8), :] = base[rows, :] * kappa
            E[2, y + 8, pl.ds(8 + 8 * xo, 8), :] = weight
        return c

    lax.fori_loop(0, 32, fill, 0)
    yc = [remote(E.at[:, pl.ds(35, 5), pl.ds(8, 32)], yr.at[0], send, recv, 7, "gy", 1),
          remote(E.at[:, pl.ds(8, 5), pl.ds(8, 32)], yr.at[1], send, recv, 8, "gy", -1)]
    lane8 = lane // 8

    def packz(n, c):
        f, q, xo = n // 8, lax.rem(n // 4, 2), lax.rem(n, 4)
        top, bottom = None, None
        for i in range(16):
            v = E[f, 8 + 16 * q + i, pl.ds(pl.multiple_of(8 + 8 * xo, 8), 8), :]
            hi = rot(v, (8 * i + 8) % 128)
            lo = rot(v, (8 * i) % 128) if i else v
            top = hi if i == 0 else jnp.where(lane8 == i, hi, top)
            bottom = lo if i == 0 else jnp.where(lane8 == i, lo, bottom)
        zs[0, f, q, pl.ds(pl.multiple_of(8 * xo, 8), 8), :] = top
        zs[1, f, q, pl.ds(pl.multiple_of(8 * xo, 8), 8), :] = bottom
        return c

    lax.fori_loop(0, 24, packz, 0)
    zc = [remote(zs.at[0], zr.at[0], send, recv, 9, "gz", 1), remote(zs.at[1], zr.at[1], send, recv, 10, "gz", -1)]
    for c in g1:
        c.wait()
    mine = pl.ds((ix * 4 + iy) * 8, 8)
    g2 = [remote(gat.at[mine], gat.at[mine], send, recv, 10 + s, "gy", s) for s in range(1, 4)]

    my, py = edges("gy")
    for c in yc:
        c.wait()

    def addy(n, c):
        f, k = n // 5, lax.rem(n, 5)
        E[f, 3 + k, pl.ds(8, 32), :] = yr[0, f, k] * my
        E[f, 40 + k, pl.ds(8, 32), :] = yr[1, f, k] * py
        return c

    lax.fori_loop(0, 15, addy, 0)

    def stage5(n, c):
        f, y = n // 42, lax.rem(n, 42)
        xs[0, pl.ds(n * 5, 5), :] = E[f, 3 + y, pl.ds(35, 5), :]
        xs[1, pl.ds(n * 5, 5), :] = E[f, 3 + y, pl.ds(8, 5), :]
        return c

    lax.fori_loop(0, 126, stage5, 0)
    xc = [remote(xs.at[0], xr.at[0], send, recv, 14, "gx", 1), remote(xs.at[1], xr.at[1], send, recv, 15, "gx", -1)]
    for c in g2:
        c.wait()
    plane = pl.ds(ix * 32, 32)
    g3 = [remote(gat.at[plane], gat.at[plane], send, recv, 15 + s, "gx", s) for s in range(1, 4)]

    mz, pz = edges("gz")
    for c in zc:
        c.wait()
    lane16 = lane // 16
    low = lax.rem(lane, 16) < 8

    def windows(n, c):
        f, xo = n // 4, lax.rem(n, 4)
        rows = pl.ds(pl.multiple_of(8 * xo, 8), 8)
        src = [[zr[d, f, q, rows, :] * m for q in range(2)] for d, m in ((0, mz), (1, pz))]
        for g in range(1, 6):
            acc = jnp.zeros((8, 128), jnp.float32)
            for pos in range(8):
                y = group_row(g, pos) - 8
                if y < 0 or y > 31:
                    continue
                a = rot(src[0][y // 16], (16 * pos - 8 * (y % 16)) % 128)
                b = rot(src[1][y // 16], (16 * pos + 8 - 8 * (y % 16)) % 128)
                acc = jnp.where(lane16 == pos, jnp.where(low, a, b), acc)
            G[f, g, pl.ds(pl.multiple_of(8 + 8 * xo, 8), 8), :] = acc
        return c

    lax.fori_loop(0, 12, windows, 0)
    wc = [remote(G.at[:, pl.ds(4, 2), pl.ds(8, 32)], yg.at[0], send, recv, 19, "gy", 1),
          remote(G.at[:, pl.ds(1, 2), pl.ds(8, 32)], yg.at[1], send, recv, 20, "gy", -1)]
    mx, px = edges("gx")
    for c in xc:
        c.wait()

    def unstage5(n, c):
        f, y = n // 42, lax.rem(n, 42)
        E[f, 3 + y, pl.ds(3, 5), :] = xr[0, pl.ds(n * 5, 5), :] * mx
        E[f, 3 + y, pl.ds(40, 5), :] = xr[1, pl.ds(n * 5, 5), :] * px
        return c

    lax.fori_loop(0, 126, unstage5, 0)
    for c in wc:
        c.wait()
    for f in range(3):
        for k in range(2):
            G[f, k, pl.ds(8, 32), :] += yg[0, f, k] * my
            G[f, 5 + k, pl.ds(8, 32), :] += yg[1, f, k] * py
    def stageg(n, c):
        f, g = n // 7, lax.rem(n, 7)
        xgs[0, pl.ds(n * 5, 5), :] = G[f, g, pl.ds(35, 5), :]
        xgs[1, pl.ds(n * 5, 5), :] = G[f, g, pl.ds(8, 5), :]
        return c
    lax.fori_loop(0, 21, stageg, 0)
    vc = [remote(xgs.at[0], xgr.at[0], send, recv, 21, "gx", 1), remote(xgs.at[1], xgr.at[1], send, recv, 22, "gx", -1)]
    for c in g3 + vc:
        c.wait()
    def unstageg(n, c):
        f, g = n // 7, lax.rem(n, 7)
        G[f, g, pl.ds(3, 5), :] = xgr[0, pl.ds(n * 5, 5), :] * mx
        G[f, g, pl.ds(40, 5), :] = xgr[1, pl.ds(n * 5, 5), :] * px
        return c
    lax.fori_loop(0, 21, unstageg, 0)


HALO = [("gy", 1), ("gy", -1), ("gx", 1), ("gx", -1), ("gz", 1), ("gz", -1)]


def split_rows(T, ey, rows):
    lane, _ = lanes_sub()
    t0 = rot(T[0, ey, rows, :], 124)
    t1 = rot(T[1, ey, rows, :], 4)
    a = jnp.where(lane < 124, t0, 0.0) + jnp.where(lane >= 4, t1, 0.0)
    m = jnp.where(lane >= 124, t0, jnp.where(lane < 4, t1, 0.0))
    return a, m


def merge_kernel(T, E, W, zs, zr, yr, yw, xs, xr, xws, xwr, send, recv):
    greet(HALO)
    lane, sub = lanes_sub()
    lane16 = lane // 16
    low = lax.rem(lane, 16) < 8
    E[...] = jnp.zeros_like(E)
    W[...] = jnp.zeros_like(W)

    def build(n, c):
        g, xo = 1 + n // 6, lax.rem(n, 6)
        rows = pl.ds(pl.multiple_of(8 * xo, 8), 8)
        nxt, prv, own = None, None, None
        for pos in range(8):
            ey = 8 * g - 4 + pos
            a, m = split_rows(T, ey, rows)
            E[ey, rows, :] = a
            ra = rot(a, (16 * pos + 8) % 128)
            rm = rot(m, (16 * pos + 8) % 128)
            s0, s1 = jnp.where(low, ra, rm), jnp.where(low, rm, ra)
            if pos == 0:
                nxt, prv, own = s0, s1, rm
            else:
                hit = lane16 == pos
                nxt, prv, own = jnp.where(hit, s0, nxt), jnp.where(hit, s1, prv), jnp.where(hit, rm, own)
        zs[0, g - 1, rows, :] = nxt
        zs[1, g - 1, rows, :] = prv
        W[0, g, rows, :] = own
        return c

    lax.fori_loop(0, 30, build, 0)
    yc = [remote(E.at[pl.ds(35, 9)], yr.at[0], send, recv, 0, "gy", 1), remote(E.at[pl.ds(4, 9)], yr.at[1], send, recv, 1, "gy", -1)]
    zc = [remote(zs.at[0], zr.at[0], send, recv, 2, "gz", 1), remote(zs.at[1], zr.at[1], send, recv, 3, "gz", -1)]
    my, py = edges("gy")
    mz, pz = edges("gz")
    mx, px = edges("gx")
    for c in yc:
        c.wait()
    def addy(k, c):
        E[3 + k] += yr[0, k] * my
        E[36 + k] += yr[1, k] * py
        return c
    lax.fori_loop(0, 9, addy, 0)
    def stage(y, c):
        xs[0, pl.ds(y * 9, 9), :] = E[3 + y, pl.ds(35, 9), :]
        xs[1, pl.ds(y * 9, 9), :] = E[3 + y, pl.ds(4, 9), :]
        return c
    lax.fori_loop(0, 42, stage, 0)
    xc = [remote(xs.at[0], xr.at[0], send, recv, 4, "gx", 1), remote(xs.at[1], xr.at[1], send, recv, 5, "gx", -1)]
    for c in zc:
        c.wait()
    def windows(n, c):
        g, xo = n // 6, lax.rem(n, 6)
        rows = pl.ds(pl.multiple_of(8 * xo, 8), 8)
        x, y = zr[0, g, rows, :] * mz, zr[1, g, rows, :] * pz
        W[0, g + 1, rows, :] += jnp.where(low, x, y)
        W[1, g + 1, rows, :] = jnp.where(low, y, x)
        return c
    lax.fori_loop(0, 30, windows, 0)
    wc = [remote(W.at[:, pl.ds(4, 2)], yw.at[0], send, recv, 6, "gy", 1), remote(W.at[:, pl.ds(1, 2)], yw.at[1], send, recv, 7, "gy", -1)]
    for c in wc:
        c.wait()
    for w in range(2):
        for k in range(2):
            W[w, k] += yw[0, w, k] * my
            W[w, 5 + k] += yw[1, w, k] * py
    def stagew(n, c):
        w, g = n // 7, lax.rem(n, 7)
        xws[0, pl.ds(n * 9, 9), :] = W[w, g, pl.ds(35, 9), :]
        xws[1, pl.ds(n * 9, 9), :] = W[w, g, pl.ds(4, 9), :]
        return c
    lax.fori_loop(0, 14, stagew, 0)
    vc = [remote(xws.at[0], xwr.at[0], send, recv, 8, "gx", 1), remote(xws.at[1], xwr.at[1], send, recv, 9, "gx", -1)]
    for c in xc:
        c.wait()
    def unstage(y, c):
        E[3 + y, pl.ds(3, 9), :] += xr[0, pl.ds(y * 9, 9), :] * mx
        E[3 + y, pl.ds(36, 9), :] += xr[1, pl.ds(y * 9, 9), :] * px
        return c
    lax.fori_loop(0, 42, unstage, 0)
    for c in vc:
        c.wait()
    def unstagew(n, c):
        w, g = n // 7, lax.rem(n, 7)
        W[w, g, pl.ds(3, 9), :] += xwr[0, pl.ds(n * 9, 9), :] * mx
        W[w, g, pl.ds(36, 9), :] += xwr[1, pl.ds(n * 9, 9), :] * px
        return c
    lax.fori_loop(0, 14, unstagew, 0)


def fold_kernel(T, C, upd, E, zs, zr, yr, xs, xr, send, recv):
    greet(HALO)
    lane, sub = lanes_sub()
    lane8 = lane // 8

    def build(n, c):
        q, xo = n // 6, lax.rem(n, 6)
        rows = pl.ds(pl.multiple_of(8 * xo, 8), 8)
        nxt, prv = None, None
        for i in range(16):
            ey = 4 + 16 * q + i
            a, m = split_rows(T, ey, rows)
            E[ey, rows, :] = a
            hi = rot(m, (8 * i) % 128) if i else m
            lo = rot(m, (8 * i + 8) % 128)
            nxt = hi if i == 0 else jnp.where(lane8 == i, hi, nxt)
            prv = lo if i == 0 else jnp.where(lane8 == i, lo, prv)
        zs[0, q, rows, :] = nxt
        zs[1, q, rows, :] = prv
        return c

    lax.fori_loop(0, 18, build, 0)
    zc = [remote(zs.at[0], zr.at[0], send, recv, 0, "gz", 1), remote(zs.at[1], zr.at[1], send, recv, 1, "gz", -1)]
    my, py = edges("gy")
    mz, pz = edges("gz")
    mx, px = edges("gx")
    for c in zc:
        c.wait()
    def addz(n, c):
        q, xo = n // 6, lax.rem(n, 6)
        rows = pl.ds(pl.multiple_of(8 * xo, 8), 8)
        x, y = zr[0, q, rows, :] * mz, zr[1, q, rows, :] * pz
        for i in range(16):
            a = rot(x, (128 - 8 * i) % 128) if i else x
            b = rot(y, (120 - 8 * i) % 128)
            E[4 + 16 * q + i, rows, :] += jnp.where(lane < 8, a, jnp.where(lane >= 120, b, 0.0))
        return c
    lax.fori_loop(0, 18, addz, 0)
    yc = [remote(E.at[pl.ds(40, 4)], yr.at[0], send, recv, 2, "gy", 1), remote(E.at[pl.ds(4, 4)], yr.at[1], send, recv, 3, "gy", -1)]
    for c in yc:
        c.wait()
    for k in range(4):
        E[8 + k] += yr[0, k] * my
        E[36 + k] += yr[1, k] * py
    def stage(y, c):
        xs[0, pl.ds(y * 4, 4), :] = E[8 + y, pl.ds(40, 4), :]
        xs[1, pl.ds(y * 4, 4), :] = E[8 + y, pl.ds(4, 4), :]
        return c
    lax.fori_loop(0, 32, stage, 0)
    xc = [remote(xs.at[0], xr.at[0], send, recv, 4, "gx", 1), remote(xs.at[1], xr.at[1], send, recv, 5, "gx", -1)]
    for c in xc:
        c.wait()
    def finish(y, c):
        E[8 + y, pl.ds(8, 4), :] += xr[0, pl.ds(y * 4, 4), :] * mx
        E[8 + y, pl.ds(36, 4), :] += xr[1, pl.ds(y * 4, 4), :] * px
        for xo in range(4):
            upd[pl.ds(xo * 256 + y, 8, stride=32), :] = C[y, pl.ds(8 * xo, 8), :] + E[8 + y, pl.ds(8 + 8 * xo, 8), :]
        return c
    lax.fori_loop(0, 32, finish, 0)


def f32(*shape):
    return jax.ShapeDtypeStruct(shape, jnp.float32)


def vmem(*shape):
    return pltpu.VMEM(shape, jnp.float32)


def params(cid):
    return pltpu.CompilerParams(collective_id=cid, has_side_effects=True, vmem_limit_bytes=BIG)


def share(coef, forcing, base, labels, con, chw):
    return pl.pallas_call(
        share_kernel, out_shape=(f32(128, 4, 128), f32(3, 48, 48, 128), f32(3, 7, 48, 128)),
        in_specs=[VM, VM, VM, VM, SM, SM], out_specs=(VM, VM, VM),
        scratch_shapes=[vmem(2, 3, 2, 32, 128), vmem(2, 3, 2, 32, 128), vmem(2, 3, 5, 32, 128), vmem(2, 3, 2, 32, 128),
                        vmem(2, 632, 128), vmem(2, 632, 128), vmem(2, 112, 128), vmem(2, 112, 128),
                        pltpu.SemaphoreType.DMA((23,)), pltpu.SemaphoreType.DMA((23,))],
        compiler_params=params(0), name="share")(coef, forcing, base, labels, con, chw)


def merge(T):
    return pl.pallas_call(
        merge_kernel, out_shape=(f32(48, 48, 128), f32(2, 7, 48, 128)), in_specs=[VM], out_specs=(VM, VM),
        scratch_shapes=[vmem(2, 5, 48, 128), vmem(2, 5, 48, 128), vmem(2, 9, 48, 128), vmem(2, 2, 2, 48, 128),
                        vmem(2, 384, 128), vmem(2, 384, 128), vmem(2, 128, 128), vmem(2, 128, 128),
                        pltpu.SemaphoreType.DMA((10,)), pltpu.SemaphoreType.DMA((10,))],
        compiler_params=params(1), name="merge")(T)


def fold(T, C):
    return pl.pallas_call(
        fold_kernel, out_shape=f32(1024, 128), in_specs=[VM, VM], out_specs=VM,
        scratch_shapes=[vmem(52, 48, 128), vmem(2, 3, 48, 128), vmem(2, 3, 48, 128), vmem(2, 4, 48, 128),
                        vmem(2, 128, 128), vmem(2, 128, 128),
                        pltpu.SemaphoreType.DMA((6,)), pltpu.SemaphoreType.DMA((6,))],
        compiler_params=params(2), name="fold")(T, C)


def prolong_kernel(live_ref, off, link, gat, basis, acc, buf, sems):
    live = jnp.clip(live_ref[0], 0, NP)

    def fetch(p):
        return pltpu.make_async_copy(basis.at[pl.ds(p * 256, 256)], buf.at[pl.ds(p * 256, 256)], sems.at[p])

    def start(p, c):
        fetch(p).start()
        return c

    lax.fori_loop(0, live, start, 0)
    acc[...] = jnp.zeros_like(acc)
    lane, sub = lanes_sub()
    ix, iy, iz = lax.axis_index("gx"), lax.axis_index("gy"), lax.axis_index("gz")

    def body(p, c):
        ox, oy, tile, lo = corner(off, p)
        owner = ((ix + link[p, 0] - 1) * 4 + iy + link[p, 1] - 1) * 8 + iz + link[p, 2] - 1
        owner = jnp.clip(owner, 0, 127)
        slot = jnp.clip(link[p, 3], 0, ND - 1)
        row = jnp.broadcast_to(gat[owner, pl.ds(slot // 16, 1), :], (8, 128))
        row = rot(row, lax.rem(128 - 8 * lax.rem(slot, 16), 128))
        ck = [jnp.broadcast_to(row[:, k : k + 1], (8, 128)) for k in range(NB)]
        fetch(p).wait()
        inwin = (lane >= lo) & (lane < lo + 16)
        for yh in range(2):
            for xo in range(2):
                v = None
                for k in range(NB):
                    t = ck[k] * buf[pl.ds(p * 256 + 128 * xo + 8 * yh + k, 8, stride=16), :]
                    v = t if v is None else v + t
                for yl in range(8):
                    r = rot(v, lax.rem(lo - 16 * yl + 128, 128))
                    acc[tile, oy + 4 + 8 * yh + yl, pl.ds(ox + 4 + 8 * xo, 8), :] += jnp.where(inwin, r, 0.0)
        return c

    lax.fori_loop(0, live, body, 0)


def residual_stage(E, G, Ec, Wc, R, K, W, gk, C, gc, inner):
    lane, sub = lanes_sub()
    near = (lane < 8) | (lane >= 120)

    def unpack(n, c):
        g, xo = n // 6, lax.rem(n, 6)
        rows = pl.ds(pl.multiple_of(8 * xo, 8), 8)
        gs, cs, ks = Wc[0, g, rows, :], Wc[1, g, rows, :], G[1, g, rows, :]
        for pos in range(8):
            ey = group_row(g, pos) + 4
            s = (120 - 16 * pos) % 128
            gc[ey, rows, :] = rot(gs, s)
            gk[ey, rows, :] = rot(ks, s)
            C[ey, rows, :] = Ec[jnp.clip(ey - 4, 0, 47), rows, :] + jnp.where(near, rot(cs, s), 0.0)
        return c

    lax.fori_loop(0, 42, unpack, 0)

    def pair(cv, kv, nc, nk):
        inside = nk > 0.0
        return jnp.where(inside, 0.5 * (kv + nk) * (cv - nc), kv * cv)

    def build(n, c):
        g, xo = 1 + n // 5, lax.rem(n, 5)
        x0 = 4 + 8 * xo
        rows, before, after = pl.ds(x0, 8), pl.ds(x0 - 1, 8), pl.ds(x0 + 1, 8)
        gf, gw = G[0, g, rows, :], G[2, g, rows, :]
        for pos in range(8):
            ey = group_row(g, pos) + 4
            s = (120 - 16 * pos) % 128
            cv, gv = C[ey, rows, :], gc[ey, rows, :]
            kv, hv = E[1, ey - 4, rows, :], gk[ey, rows, :]
            cu, cd, gu, gd = rot(cv, 127), rot(cv, 1), rot(gv, 127), rot(gv, 1)
            ku, kd, hu, hd = rot(kv, 127), rot(kv, 1), rot(hv, 127), rot(hv, 1)
            last, first = lane == 127, lane == 0
            r = E[0, ey - 4, rows, :]
            r = r - pair(cv, kv, jnp.where(last, gu, cu), jnp.where(last, hu, ku))
            r = r - pair(cv, kv, jnp.where(first, gd, cd), jnp.where(first, hd, kd))
            q = rot(gf, s)
            q = q - pair(gv, hv, jnp.where(last, cu, gu), jnp.where(last, ku, hu))
            q = q - pair(gv, hv, jnp.where(first, cd, gd), jnp.where(first, kd, hd))
            for dy, rr in ((-1, rows), (1, rows), (0, before), (0, after)):
                r = r - pair(cv, kv, C[ey + dy, rr, :], E[1, ey - 4 + dy, rr, :])
                q = q - pair(gv, hv, gc[ey + dy, rr, :], gk[ey + dy, rr, :])
            head, tail = lane < 4, lane >= 124
            py, px = ey - 8, pl.ds(pl.multiple_of(8 * xo, 8), 8)
            wv = E[2, ey - 4, rows, :]
            R[0, py, px, :] = jnp.where(head, rot(q, 4), rot(r, 4))
            R[1, py, px, :] = jnp.where(tail, rot(q, 124), rot(r, 124))
            K[0, py, px, :] = jnp.where(head, rot(hv, 4), rot(kv, 4))
            K[1, py, px, :] = jnp.where(tail, rot(hv, 124), rot(kv, 124))
            W[0, py, px, :] = jnp.where(head, rot(gw, (s + 4) % 128), rot(wv, 4))
            W[1, py, px, :] = jnp.where(tail, rot(gw, (s + 124) % 128), rot(wv, 124))
        return c

    lax.fori_loop(0, 25, build, 0)

    def keep(y, c):
        inner[y] = C[y + 12, pl.ds(8, 32), :]
        return c

    lax.fori_loop(0, 32, keep, 0)


def enrich_kernel(live_ref, off, E, G, Ec, Wc, out, corr, inner, R, K, W, gk, C, gc, cbuf, vbuf):
    residual_stage(E, G, Ec, Wc, R, K, W, gk, C, gc, inner)
    live = jnp.clip(live_ref[0], 0, NP)
    corr[...] = jnp.zeros_like(corr)
    lane, sub = lanes_sub()
    group = lane // 16
    zpos = lane % 16
    zw = zpos < 15
    zg = zpos > 0
    yup = lane < 112
    ydn = lane >= 16
    xup = sub < 7
    xdn = sub > 0
    fz = zpos.astype(jnp.float32)
    def tentf(t):
        return (t + 0.5) * (PIECE - t - 0.5) * (4.0 / (PIECE * PIECE))
    tents = {}
    for xp in range(2):
        for yp in range(2):
            tents[xp, yp] = tentf((2*sub + xp).astype(jnp.float32)) * tentf((2*group + yp).astype(jnp.float32)) * tentf(fz)
    par = [(0,0),(0,1),(1,0),(1,1)]

    def prep(p, slot):
        ox, oy, tile, lo = corner(off, p)
        active = jnp.where(p < live, 1.0, 0.0)
        got = []
        for F in (R, K, W):
            d = {}
            for xp, yp in par:
                a = None
                for yh in range(8):
                    row = F[tile, oy + 2*yh + yp, pl.ds(ox + xp, 8, stride=2), :]
                    r = rot(row, lax.rem(16*yh - lo + 128, 128))
                    a = r if a is None else jnp.where(group == yh, r, a)
                d[xp, yp] = a
            got.append(d)
        r, k, w = got
        for i, (xp, yp) in enumerate(par):
            kc = k[xp, yp]
            nbs = [
                (rot(kc, 127), zw), (rot(kc, 1), zg),
                (k[xp, 1-yp], None),
                (rot(k[xp, 1-yp], 16 if yp == 0 else 112), ydn if yp == 0 else yup),
                (k[1-xp, yp], None),
                (rot(k[1-xp, yp], 1 if xp == 0 else 7, 0), xdn if xp == 0 else xup),
            ]
            diag = None
            cs = []
            inside = kc > 0.0
            for nb, m in nbs:
                ok = nb > 0.0
                if m is not None:
                    ok = ok & m
                face = jnp.where(ok, 0.5 * (kc + nb), kc)
                cs.append(jnp.where(ok & inside, face, 0.0))
                diag = face if diag is None else diag + face
            inv = jnp.where(inside, OMEGA / jnp.where(inside, diag, 1.0), 0.0)
            for j, cj in enumerate(cs):
                cbuf[slot, pl.ds((i*6 + j)*8, 8), :] = cj * inv
            b1 = r[xp, yp] * inv * active
            vbuf[slot, pl.ds(i*8, 8), :] = b1
            vbuf[slot, pl.ds((4+i)*8, 8), :] = b1 * w[xp, yp]

    def sweep_piece(vs, slot):
        res = []
        for s in range(2):
            v = {par[i]: vs[s*4+i] for i in range(4)}
            for i, (xp, yp) in enumerate(par):
                c = [cbuf[slot, pl.ds((i*6 + j)*8, 8), :] for j in range(6)]
                vc = v[xp, yp]
                t0 = vbuf[slot, pl.ds((4*s+i)*8, 8), :] + (1.0 - OMEGA) * vc
                t1 = c[0] * rot(vc, 127) + c[1] * rot(vc, 1)
                t2 = c[2] * v[xp, 1-yp] + c[3] * rot(v[xp, 1-yp], 16 if yp == 0 else 112)
                t3 = c[4] * v[1-xp, yp] + c[5] * rot(v[1-xp, yp], 1 if xp == 0 else 7, 0)
                res.append((t0 + t1) + (t2 + t3))
        return res

    idxs = [16*(4*yh2 + group//2) + zpos for yh2 in range(2)]
    gpar = (group % 2) == 0

    def body(g, c):
        for slot in range(PAIR):
            prep(g*PAIR + slot, slot)
        init = tuple(vbuf[slot, pl.ds(n*8, 8), :] for slot in range(PAIR) for n in range(8))
        def sweep(_, vs):
            o = []
            for slot in range(PAIR):
                o += sweep_piece(vs[slot*8:slot*8+8], slot)
            return tuple(o)
        vs = lax.fori_loop(0, SWEEPS - 1, sweep, init)
        for slot in range(PAIR):
            p = g*PAIR + slot
            ox, oy, tile, lo = corner(off, p)
            inwin = (lane >= lo) & (lane < lo + 16)
            v = vs[slot*8:slot*8+8]
            for s in range(2):
                for xp in range(2):
                    for yh2 in range(2):
                        e = jnp.take_along_axis(v[s*4 + 2*xp], idxs[yh2], axis=1)
                        o = jnp.take_along_axis(v[s*4 + 2*xp + 1], idxs[yh2], axis=1)
                        out[pl.ds(p*64 + 4*xp + 2*yh2 + s, 8, stride=8), :] = jnp.where(gpar, e, o)
            for i, (xp, yp) in enumerate(par):
                sp = tents[xp, yp] * (v[i] + v[4+i])
                for yh in range(8):
                    rr = jnp.where(inwin, rot(sp, lax.rem(lo - 16*yh + 128, 128)), 0.0)
                    corr[tile, oy + 4 + 2*yh + yp, pl.ds(ox + 4 + xp, 8, stride=2), :] += rr
        return c
    ng = (live + PAIR - 1) // PAIR
    lax.fori_loop(0, ng, body, 0)
    def zero(p, c):
        out[pl.ds(p*64, 64), :] = jnp.zeros((64, 128), jnp.float32)
        return c
    lax.fori_loop(ng*PAIR, NP, zero, 0)


def prolong(live, off, link, gat, basis):
    return pl.pallas_call(
        prolong_kernel, out_shape=f32(2, 52, 48, 128), in_specs=[SM, SM, SM, VM, ANY], out_specs=VM,
        scratch_shapes=[vmem(NP * 256, 128), pltpu.SemaphoreType.DMA((NP,))],
        compiler_params=pltpu.CompilerParams(vmem_limit_bytes=BIG), name="prolong")(live, off, link, gat, basis)


def enrich(live, off, E, G, Ec, Wc):
    return pl.pallas_call(
        enrich_kernel, out_shape=(f32(NP * 64, 128), f32(2, 52, 48, 128), f32(32, 32, 128)),
        in_specs=[SM, SM, VM, VM, VM, VM], out_specs=(VM, VM, VM),
        scratch_shapes=[vmem(2, 40, 40, 128), vmem(2, 40, 40, 128), vmem(2, 40, 40, 128),
                        vmem(56, 48, 128), vmem(56, 48, 128), vmem(56, 48, 128), vmem(PAIR, 192, 128), vmem(PAIR, 64, 128)],
        compiler_params=pltpu.CompilerParams(vmem_limit_bytes=BIG), name="enrich")(live, off, E, G, Ec, Wc)


def basis_rows(rb):
    return rb.reshape(NP, NB, 32, 128).transpose(0, 2, 1, 3).reshape(NP * 256, 128)


def out_basis(o):
    return o.reshape(NP, 32, 2, 128).transpose(0, 2, 1, 3).reshape(1, 1, 1, NP, 2, 4096)


def local(forcing, kappa_base, labels, contrast, channel_weight, coarse_coef, source_link, offsets, live_pieces, resident_bases):
    live = live_pieces.reshape(1)
    off = offsets[0, 0, 0]
    link = source_link[0, 0, 0]
    gat, E, G = share(
        coarse_coef.reshape(1, 4, 128), forcing.reshape(1024, 128), kappa_base.reshape(1024, 128), labels.reshape(1024, 128),
        contrast, channel_weight)
    T = prolong(live, off, link, gat, basis_rows(resident_bases))
    Ec, Wc = merge(T)
    out, corr, inner = enrich(live, off, E, G, Ec, Wc)
    return fold(corr, inner).reshape(32, 32, 128), out_basis(out)


def solution(mesh):
    return jax.shard_map(
        local,
        mesh=mesh,
        in_specs=(
            P("gx", "gy", "gz"),
            P("gx", "gy", "gz"),
            P("gx", "gy", "gz"),
            P(),
            P(),
            P("gx", "gy", "gz", None, None),
            P("gx", "gy", "gz", None, None),
            P("gx", "gy", "gz", None, None),
            P("gx", "gy", "gz"),
            P("gx", "gy", "gz", None, None, None),
        ),
        out_specs=(P("gx", "gy", "gz"), P("gx", "gy", "gz", None, None, None)),
        check_vma=False,
    )
```

time: 671 us -> 179 us (0.27)
  the two profiles are of different devices: /device:TPU:41 before, /device:TPU:64 now
where the time goes in v2:
time: 179 us; the launch traced here: 175 us
  Pallas kernels  168 us (94%)
  local copies, waits for them, and re-layouts  6.04 us (3%)
    pallas_call x1, Pallas kernels, fold(): pl.pallas_call(fold_kernel, out_shape=f32(1024, 128), in_specs=[VM, VM],...  50.3 us
    pallas_call x1, Pallas kernels, enrich(): pl.pallas_call(enrich_kernel, out_shape=(f32(NP * 64, 128), f32(2, 52, 48...  44.2 us
    pallas_call x1, Pallas kernels, share(): pl.pallas_call(share_kernel, out_shape=(f32(128, 4, 128), f32(3, 48, 48,...  35 us
    pallas_call x1, Pallas kernels, merge(): pl.pallas_call(merge_kernel, out_shape=(f32(48, 48, 128), f32(2, 7, 48, 1...  29.9 us
    pallas_call x1, Pallas kernels, prolong(): pl.pallas_call(prolong_kernel, out_shape=f32(2, 52, 48, 128), in_specs=[S...  8.7 us
    unnamed x3, local copies, waits for them, and re-layouts  4.01 us

profile of v2, /device:TPU:64, one launch (start us, length us, event | category | flops | bytes accessed | tf_op | source)
XLA Modules:
  0.0 175.4 jit_solution(11405810251073350100)
XLA Ops:
  1.3 1.4 copy.18
  2.6 1.4 copy.22
  4.0 0.8 copy.17
  4.8 0.7 reshape.35.coef
  5.4 35.0 %share.1 = (f32[128,4,128]{2,1,0:T(4,128)}, f32[3,48,48,128]{3,2,1,0:T(8,128)}, f32[3,7,48,128]{3,2,1,0:T(8,128)}) custom-call(f32[1,4,128]{2,1,0:T(4,128)} %reshape.35.coef, f32[1024,128]{1,0:T(8,128)} %bitcast.23, f32[1024,128]{1,0:T(8,128)} %bitcast.24, s32[1024,128]{1,0:T(8,128)} %bitcast.25, f32[4]{0:T(128)} %con.1, f32[4]{0:T(128)} %chw.1), custom_call_target="tpu_custom_call" | custom-call | tf_op jit(solution)/shard_map/share/pallas_call | solution.py:373
  40.4 8.7 %prolong.1.T = f32[2,52,48,128]{3,2,1,0:T(8,128)} custom-call(s32[1]{0:T(128)} %bitcast.19.live_ref, s32[40,3]{1,0:T(8,128)} %bitcast.26, s32[40,4]{1,0:T(8,128)} %bitcast.28, f32[128,4,128]{2,1,0:T(4,128)} %get-tuple-element.12.gat, f32[10240,128]{1,0:T(8,128)} %bitcast.21), custom_call_target="tpu_custom_call" | custom-call | tf_op jit(solution)/shard_map/prolong/pallas_call | solution.py:619
  49.1 29.9 %merge.1 = (f32[48,48,128]{2,1,0:T(8,128)}, f32[2,7,48,128]{3,2,1,0:T(8,128)}) custom-call(f32[2,52,48,128]{3,2,1,0:T(8,128)} %prolong.1.T), custom_call_target="tpu_custom_call" | custom-call | tf_op jit(solution)/shard_map/merge/pallas_call | solution.py:383
  79.0 44.2 %enrich.1 = (f32[2560,128]{1,0:T(8,128)}, f32[2,52,48,128]{3,2,1,0:T(8,128)}, f32[32,32,128]{2,1,0:T(8,128)}) custom-call(s32[1]{0:T(128)} %bitcast.20.live_ref, s32[40,3]{1,0:T(8,128)} %bitcast.27, f32[3,48,48,128]{3,2,1,0:T(8,128)} %get-tuple-element.10.E, f32[3,7,48,128]{3,2,1,0:T(8,128)} %get-tuple-element.11.G, f32[48,48,128]{2,1,0:T(8,128)} %get-tuple-element.13.Ec, ...), custom_call_target="tpu_custom_call" | custom-call | tf_op jit(solution)/shard_map/enrich/pallas_call | solution.py:626
  123.2 50.3 %fold.1 = f32[1024,128]{1,0:T(8,128)} custom-call(f32[2,52,48,128]{3,2,1,0:T(8,128)} %get-tuple-element.15.T, f32[32,32,128]{2,1,0:T(8,128)} %get-tuple-element.16.C), custom_call_target="tpu_custom_call" | custom-call | tf_op jit(solution)/shard_map/fold/pallas_call | solution.py:392
  173.5 1.9 %copy.25 = f32[32,32,128]{2,1,0:T(8,128)} copy(f32[32,32,128]{2,1,0:T(8,128)} %bitcast.22) | data formatting | bytes 1048576
